TPU v7x, 32 devices: a whole 2x2x4 slice. The times are simulated.
32 devices in a mesh: rep: 2 (over y), shard: 16 (over z, x, core).
Axes of the slice: x: 2, y: 2, z: 4, core: 2. Of those that a mesh axis runs over, the one named last changes fastest.
Arguments:
- latents: bfloat16 [32, 128, 1152], P(('rep', 'shard')), may hold values from -5 to 5
- cond: float32 [32, 1152], P(('rep', 'shard')), may hold values from -6 to 6
- timesteps: int32 [32], P(('rep', 'shard')), may hold values from 0 to 999
- cotangent: bfloat16 [32, 128, 1152], P(('rep', 'shard')), may hold values from -6 to 6
- w_qkv: float32 [1152, 3456], P('shard'), may hold values from -0.11785113 to 0.11785113
- w_proj: float32 [1152, 1152], P('shard'), may hold values from -0.75 to 0.75
- w_fc1: float32 [1152, 4608], P('shard'), may hold values from -0.1875 to 0.1875
- w_fc2: float32 [4608, 1152], P('shard'), may hold values from -0.1875 to 0.1875
- w_ada: float32 [1152, 6912], P(None, 'shard'), may hold values from -0.015625 to 0.015625
- biases: float32 [16128], replicated, may hold values from -3 to 3
- m_qkv: float32 [1152, 3456], P('shard', 'rep'), may hold values from -0.00012272017 to 0.00012272017
- m_proj: float32 [1152, 1152], P('shard', 'rep'), may hold values from -0.00012272017 to 0.00012272017
- m_fc1: float32 [1152, 4608], P('shard', 'rep'), may hold values from -0.00012272017 to 0.00012272017
- m_fc2: float32 [4608, 1152], P('shard', 'rep'), may hold values from -0.00012272017 to 0.00012272017
- m_ada: float32 [1152, 6912], P('rep', 'shard'), may hold values from -0.00012272017 to 0.00012272017
- m_bias: float32 [16128], replicated, may hold values from -0.00012272017 to 0.00012272017
- v_qkv: float32 [1152, 3456], P('shard', 'rep'), may hold values from 4.1834e-11 to 1.67336e-10
- v_proj: float32 [1152, 1152], P('shard', 'rep'), may hold values from 4.1834e-11 to 1.67336e-10
- v_fc1: float32 [1152, 4608], P('shard', 'rep'), may hold values from 4.1834e-11 to 1.67336e-10
- v_fc2: float32 [4608, 1152], P('shard', 'rep'), may hold values from 4.1834e-11 to 1.67336e-10
- v_ada: float32 [1152, 6912], P('rep', 'shard'), may hold values from 4.1834e-11 to 1.67336e-10
- v_bias: float32 [16128], replicated, may hold values from 4.1834e-11 to 1.67336e-10
Outputs:
- block_out: float32 [32, 128, 1152], P(('rep', 'shard'))
- latents_grad: float32 [32, 128, 1152], P(('rep', 'shard'))
- cond_grad: float32 [32, 1152], P(('rep', 'shard'))
- new_qkv: float32 [1152, 3456], P('shard')
- new_proj: float32 [1152, 1152], P('shard')
- new_fc1: float32 [1152, 4608], P('shard')
- new_fc2: float32 [4608, 1152], P('shard')
- new_ada: float32 [1152, 6912], P(None, 'shard')
- bias_update: float32 [16128], replicated
- new_m_qkv: float32 [1152, 3456], P('shard', 'rep')
- new_m_proj: float32 [1152, 1152], P('shard', 'rep')
- new_m_fc1: float32 [1152, 4608], P('shard', 'rep')
- new_m_fc2: float32 [4608, 1152], P('shard', 'rep')
- new_m_ada: float32 [1152, 6912], P('rep', 'shard')
- new_m_bias: float32 [16128], replicated
- new_v_qkv: float32 [1152, 3456], P('shard', 'rep')
- new_v_proj: float32 [1152, 1152], P('shard', 'rep')
- new_v_fc1: float32 [1152, 4608], P('shard', 'rep')
- new_v_fc2: float32 [4608, 1152], P('shard', 'rep')
- new_v_ada: float32 [1152, 6912], P('rep', 'shard')
- new_v_bias: float32 [16128], replicated
All inputs are finite; a program needn't handle non-finite values.
Results may differ from a plain program's by a relative error of at most 0.014.
Values may be sent and summed in bfloat16 or wider, within the bound.
No kernel may reach another device: no remote copies, remote signals or barrier semaphores. Data moves between devices by JAX's collectives and lax.ppermute only.
A program may use at most 256 MiB of HBM per device.

v0:
```python
import math

import jax
import jax.numpy as jnp
from jax import lax
from jax.sharding import PartitionSpec as P

HD = 72
H = 16
FF = 4608


ln_eps = 1e-06
beta_one = 0.9
beta_two = 0.999
adam_eps = 1e-08
learn_rate = 0.03
decay_rate = 0.01
step_count = 2
gelu_coef = 0.044715


def product(form, left, right):
    return jnp.einsum(form, left, right, preferred_element_type=jnp.float32)


def normalize(rows):
    center = rows - jnp.mean(rows, axis=-1, keepdims=True)
    rstd = lax.rsqrt(jnp.mean(center * center, axis=-1, keepdims=True) + ln_eps)
    return (center * rstd, rstd)


def norm_back(grad, normed, rstd):
    return rstd * (
        grad
        - jnp.mean(grad, axis=-1, keepdims=True)
        - normed * jnp.mean(grad * normed, axis=-1, keepdims=True)
    )


def gelu_parts(pre):
    root = math.sqrt(2.0 / math.pi)
    inner = root * (pre + gelu_coef * pre * pre * pre)
    tangent = jnp.tanh(inner)
    value = 0.5 * pre * (1.0 + tangent)
    slope = 0.5 * (1.0 + tangent) + 0.5 * pre * (1.0 - tangent * tangent) * root * (
        1.0 + 3.0 * gelu_coef * pre * pre
    )
    return (value, slope)


def time_embed(steps, width):
    half = width // 2
    freqs = jnp.exp(-math.log(10000.0) * jnp.arange(half, dtype=jnp.float32) / half)
    angles = steps.astype(jnp.float32)[:, None] * freqs[None, :]
    return jnp.concatenate([jnp.cos(angles), jnp.sin(angles)], axis=1)


def block_pass(inputs, cotan, mod, wq_b, wp_b, w1_b, w2_b, biases):
    batch, length, width = inputs.shape
    inner = H * HD
    b_q = biases[0:inner]
    b_v = biases[inner : 2 * inner]
    b_proj = biases[2 * inner : 2 * inner + width]
    b_fc1 = biases[2 * inner + width : 2 * inner + width + FF]
    b_fc2 = biases[2 * inner + width + FF : 2 * inner + 2 * width + FF]
    parts = [mod[:, i * width : (i + 1) * width][:, None, :] for i in range(6)]
    shift1, scale1, gate1, shift2, scale2, gate2 = parts
    rows = inputs.astype(jnp.float32)
    n_one, r_one = normalize(rows)
    a_one = (n_one * (1.0 + scale1) + shift1).astype(jnp.bfloat16)
    qkv = product("bld,de->ble", a_one, wq_b)
    queries = (qkv[..., :inner] + b_q).astype(jnp.bfloat16).reshape(batch, length, H, HD)
    key_rows = qkv[..., inner : 2 * inner].astype(jnp.bfloat16).reshape(batch, length, H, HD)
    value_rows = (qkv[..., 2 * inner :] + b_v).astype(jnp.bfloat16).reshape(batch, length, H, HD)
    factor = HD ** (-0.5)
    scores = product("bqhd,bkhd->bhqk", queries, key_rows) * factor
    top = jnp.max(scores, axis=-1, keepdims=True)
    expo = jnp.exp(scores - top)
    probs = expo / jnp.sum(expo, axis=-1, keepdims=True)
    probs_b = probs.astype(jnp.bfloat16)
    heads_out = product("bhqk,bkhd->bqhd", probs_b, value_rows).astype(jnp.bfloat16)
    heads_flat = heads_out.reshape(batch, length, inner)
    attn = product("ble,ed->bld", heads_flat, wp_b) + b_proj
    x_one = rows + gate1 * attn
    n_two, r_two = normalize(x_one)
    a_two = (n_two * (1.0 + scale2) + shift2).astype(jnp.bfloat16)
    pre = product("bld,df->blf", a_two, w1_b) + b_fc1
    act_val, act_slope = gelu_parts(pre)
    act = act_val.astype(jnp.bfloat16)
    mlp = product("blf,fd->bld", act, w2_b) + b_fc2
    out = x_one + gate2 * mlp
    grad_out = cotan.astype(jnp.float32)
    d_gate2 = jnp.sum(grad_out * mlp, axis=1)
    d_mlp = grad_out * gate2
    d_mlp_b = d_mlp.astype(jnp.bfloat16)
    g_fc2 = product("blf,bld->fd", act, d_mlp_b)
    g_b_fc2 = jnp.sum(d_mlp, axis=(0, 1))
    d_pre = product("bld,fd->blf", d_mlp_b, w2_b) * act_slope
    d_pre_b = d_pre.astype(jnp.bfloat16)
    g_fc1 = product("bld,blf->df", a_two, d_pre_b)
    g_b_fc1 = jnp.sum(d_pre, axis=(0, 1))
    d_a2 = product("blf,df->bld", d_pre_b, w1_b)
    d_shift2 = jnp.sum(d_a2, axis=1)
    d_scale2 = jnp.sum(d_a2 * n_two, axis=1)
    dx_one = grad_out + norm_back(d_a2 * (1.0 + scale2), n_two, r_two)
    d_gate1 = jnp.sum(dx_one * attn, axis=1)
    d_attn = dx_one * gate1
    d_attn_b = d_attn.astype(jnp.bfloat16)
    g_proj = product("ble,bld->ed", heads_flat, d_attn_b)
    g_b_proj = jnp.sum(d_attn, axis=(0, 1))
    d_heads = (
        product("bld,ed->ble", d_attn_b, wp_b).astype(jnp.bfloat16).reshape(batch, length, H, HD)
    )
    delta = jnp.sum(d_heads.astype(jnp.float32) * heads_out.astype(jnp.float32), axis=-1)
    delta = jnp.transpose(delta, (0, 2, 1))[..., None]
    d_probs = product("bqhd,bkhd->bhqk", d_heads, value_rows)
    d_scores = (probs * (d_probs - delta) * factor).astype(jnp.bfloat16)
    d_q = product("bhqk,bkhd->bqhd", d_scores, key_rows)
    d_k = product("bhqk,bqhd->bkhd", d_scores, queries)
    d_v = product("bhqk,bqhd->bkhd", probs_b, d_heads)
    g_b_q = jnp.sum(d_q, axis=(0, 1)).reshape(inner)
    g_b_v = jnp.sum(d_v, axis=(0, 1)).reshape(inner)
    d_qkv = jnp.concatenate(
        [
            d_q.reshape(batch, length, inner),
            d_k.reshape(batch, length, inner),
            d_v.reshape(batch, length, inner),
        ],
        axis=-1,
    ).astype(jnp.bfloat16)
    g_qkv = product("bld,ble->de", a_one, d_qkv)
    d_a1 = product("ble,de->bld", d_qkv, wq_b)
    d_shift1 = jnp.sum(d_a1, axis=1)
    d_scale1 = jnp.sum(d_a1 * n_one, axis=1)
    d_input = dx_one + norm_back(d_a1 * (1.0 + scale1), n_one, r_one)
    d_mod = jnp.concatenate([d_shift1, d_scale1, d_gate1, d_shift2, d_scale2, d_gate2], axis=1)
    bias_grad = jnp.concatenate([g_b_q, g_b_v, g_b_proj, g_b_fc1, g_b_fc2])
    return (out, d_input, d_mod, (g_qkv, g_proj, g_fc1, g_fc2), bias_grad)


def adam_change(weight, grad, first, second, clip):
    scaled = grad * clip
    first_new = beta_one * first + (1.0 - beta_one) * scaled
    second_new = beta_two * second + (1.0 - beta_two) * scaled * scaled
    first_hat = first_new / (1.0 - beta_one**step_count)
    second_hat = second_new / (1.0 - beta_two**step_count)
    change = -learn_rate * (first_hat / (jnp.sqrt(second_hat) + adam_eps) + decay_rate * weight)
    return (change, first_new, second_new)


def adam_step(weight, grad, first, second, clip):
    change, first_new, second_new = adam_change(weight, grad, first, second, clip)
    return (weight + change, first_new, second_new)


def shards(
    latents,
    cond,
    timesteps,
    cotangent,
    w_qkv,
    w_proj,
    w_fc1,
    w_fc2,
    w_ada,
    biases,
    m_qkv,
    m_proj,
    m_fc1,
    m_fc2,
    m_ada,
    m_bias,
    v_qkv,
    v_proj,
    v_fc1,
    v_fc2,
    v_ada,
    v_bias,
):
    width = cond.shape[1]
    b_ada = biases[biases.shape[0] - 6 * width :]
    cvec = cond + time_embed(timesteps, width)
    silu_c = jax.nn.silu(cvec).astype(jnp.bfloat16)
    ada_local = w_ada.astype(jnp.bfloat16)
    silu_group = lax.all_gather(silu_c, "shard", axis=0, tiled=True)
    mod_cols = jnp.dot(silu_group, ada_local, preferred_element_type=jnp.float32)
    mod = lax.all_to_all(mod_cols, "shard", split_axis=0, concat_axis=1, tiled=True) + b_ada
    wq_b, wp_b = (
        lax.all_gather(w_qkv.astype(jnp.bfloat16), "shard", axis=0, tiled=True),
        lax.all_gather(w_proj.astype(jnp.bfloat16), "shard", axis=0, tiled=True),
    )
    w1_b, w2_b = (
        lax.all_gather(w_fc1.astype(jnp.bfloat16), "shard", axis=0, tiled=True),
        lax.all_gather(w_fc2.astype(jnp.bfloat16), "shard", axis=0, tiled=True),
    )
    block_out, latents_grad, d_mod, grads, bias_head = block_pass(
        latents, cotangent, mod, wq_b, wp_b, w1_b, w2_b, biases
    )
    d_mod_b = d_mod.astype(jnp.bfloat16)
    d_mod_cols = lax.all_to_all(d_mod_b, "shard", split_axis=1, concat_axis=0, tiled=True)
    g_ada = jnp.dot(silu_group.T, d_mod_cols, preferred_element_type=jnp.float32)
    silu_terms = jnp.dot(d_mod_cols, ada_local.T, preferred_element_type=jnp.float32)
    silu_grad = lax.psum_scatter(silu_terms, "shard", scatter_dimension=0, tiled=True)
    sig = jax.nn.sigmoid(cvec)
    cond_grad = silu_grad * sig * (1.0 + cvec * (1.0 - sig))
    g_qkv, g_proj = (
        lax.psum_scatter(
            grads[0].astype(jnp.bfloat16), "shard", scatter_dimension=0, tiled=True
        ).astype(jnp.float32),
        lax.psum_scatter(
            grads[1].astype(jnp.bfloat16), "shard", scatter_dimension=0, tiled=True
        ).astype(jnp.float32),
    )
    g_fc1, g_fc2 = (
        lax.psum_scatter(
            grads[2].astype(jnp.bfloat16), "shard", scatter_dimension=0, tiled=True
        ).astype(jnp.float32),
        lax.psum_scatter(
            grads[3].astype(jnp.bfloat16), "shard", scatter_dimension=0, tiled=True
        ).astype(jnp.float32),
    )
    pieces = (
        lax.psum_scatter(g_qkv, "rep", scatter_dimension=1, tiled=True),
        lax.psum_scatter(g_proj, "rep", scatter_dimension=1, tiled=True),
        lax.psum_scatter(g_fc1, "rep", scatter_dimension=1, tiled=True),
        lax.psum_scatter(g_fc2, "rep", scatter_dimension=1, tiled=True),
        lax.psum_scatter(g_ada, "rep", scatter_dimension=0, tiled=True),
    )
    bias_partial = jnp.concatenate([bias_head, jnp.sum(d_mod, axis=0)])
    weight_squares = sum((jnp.sum(p * p) for p in pieces))
    g_bias, total_squares = lax.psum((bias_partial, weight_squares), ("rep", "shard"))
    gnorm = jnp.sqrt(total_squares + jnp.sum(g_bias * g_bias))
    clip = 1.0 / jnp.maximum(gnorm, 1.0)
    rank = lax.axis_index("rep")
    replicas = lax.axis_size("rep")
    weights = (w_qkv, w_proj, w_fc1, w_fc2, w_ada)
    dims = (1, 1, 1, 1, 0)
    firsts = (m_qkv, m_proj, m_fc1, m_fc2, m_ada)
    seconds = (v_qkv, v_proj, v_fc1, v_fc2, v_ada)
    new_pieces = []
    new_m = []
    new_v = []
    for weight, dim, grad, first, second in zip(weights, dims, pieces, firsts, seconds):
        count = weight.shape[dim] // replicas
        own = lax.dynamic_slice_in_dim(weight, rank * count, count, dim)
        updated, first_new, second_new = adam_step(own, grad, first, second, clip)
        new_pieces.append(updated)
        new_m.append(first_new)
        new_v.append(second_new)
    new_qkv, new_proj, new_fc1, new_fc2, new_ada = (
        lax.all_gather(new_pieces[0], "rep", axis=1, tiled=True),
        lax.all_gather(new_pieces[1], "rep", axis=1, tiled=True),
        lax.all_gather(new_pieces[2], "rep", axis=1, tiled=True),
        lax.all_gather(new_pieces[3], "rep", axis=1, tiled=True),
        lax.all_gather(new_pieces[4], "rep", axis=0, tiled=True),
    )
    bias_update, new_m_bias, new_v_bias = adam_change(biases, g_bias, m_bias, v_bias, clip)
    return (
        block_out,
        latents_grad,
        cond_grad,
        new_qkv,
        new_proj,
        new_fc1,
        new_fc2,
        new_ada,
        bias_update,
        new_m[0],
        new_m[1],
        new_m[2],
        new_m[3],
        new_m[4],
        new_m_bias,
        new_v[0],
        new_v[1],
        new_v[2],
        new_v[3],
        new_v[4],
        new_v_bias,
    )


def solution(mesh):
    in_specs = (
        P(("rep", "shard"), None, None),
        P(("rep", "shard"), None),
        P(("rep", "shard")),
        P(("rep", "shard"), None, None),
        P("shard", None),
        P("shard", None),
        P("shard", None),
        P("shard", None),
        P(None, "shard"),
        P(),
        P("shard", "rep"),
        P("shard", "rep"),
        P("shard", "rep"),
        P("shard", "rep"),
        P("rep", "shard"),
        P(),
        P("shard", "rep"),
        P("shard", "rep"),
        P("shard", "rep"),
        P("shard", "rep"),
        P("rep", "shard"),
        P(),
    )
    out_specs = (
        P(("rep", "shard"), None, None),
        P(("rep", "shard"), None, None),
        P(("rep", "shard"), None),
        P("shard", None),
        P("shard", None),
        P("shard", None),
        P("shard", None),
        P(None, "shard"),
        P(),
        P("shard", "rep"),
        P("shard", "rep"),
        P("shard", "rep"),
        P("shard", "rep"),
        P("rep", "shard"),
        P(),
        P("shard", "rep"),
        P("shard", "rep"),
        P("shard", "rep"),
        P("shard", "rep"),
        P("rep", "shard"),
        P(),
    )
    return jax.shard_map(shards, mesh=mesh, in_specs=in_specs, out_specs=out_specs, check_vma=False)
```

profile of v0, /device:TPU:0, one launch (start us, length us, event | category | flops | bytes accessed | tf_op | source)
XLA Modules:
  0.0 1095.5 jit_solution(5412278712987913531)
XLA Ops:
  11.1 2.4 convert_element_type.150
  17.3 24.2 %all-gather = bf16[16,1,1152]{2,1,0:T(2,128)(2,1)S(1)} all-gather(bf16[1,1,1152]{2,1,0:T(2,128)(2,1)S(1)} %get-tuple-element.62), channel_id=1, replica_groups=mesh['rep'=2,'shard'=16] {'shard'}, dimensions={0}, use_global_device_ids=true | all-gather | bytes 39168 | tf_op jit(solution)/shard_map/all_gather | solution.py:186
  42.8 3.5 all-to-all-start
  48.0 5.4 all-to-all-done
  54.2 31.5 %all-gather.13.cloned.1.call-done = bf16[1152,3456]{1,0:T(8,128)(2,1)} async-done(((bf16[72,3456]{1,0:T(8,128)(2,1)}), bf16[1152,3456]{1,0:T(8,128)(2,1)}) %all-gather.13.cloned.1.call-update) | async-done | bytes 7962640 | tf_op jit(solution)/shard_map/all_gather | solution.py:190
  85.7 4.7 convolution_bitcast_fusion
  92.1 38.2 %all-gather.15.cloned.1.call-done = bf16[1152,1152]{1,0:T(8,128)(2,1)} async-done(((bf16[72,1152]{1,0:T(8,128)(2,1)}), bf16[1152,1152]{1,0:T(8,128)(2,1)}) %all-gather.15.cloned.1.call-update) | async-done | bytes 2654224 | tf_op jit(solution)/shard_map/all_gather | solution.py:191
  130.3 3.2 fusion.88
  134.3 86.1 %all-gather.17.cloned.1.call-done = bf16[1152,4608]{1,0:T(8,128)(2,1)} async-done(((bf16[72,4608]{1,0:T(8,128)(2,1)}), bf16[1152,4608]{1,0:T(8,128)(2,1)}) %all-gather.17.cloned.1.call-update) | async-done | bytes 10616848 | tf_op jit(solution)/shard_map/all_gather | solution.py:194
  220.4 5.8 convolution_add_fusion
  226.2 83.5 %all-gather.19.cloned.1.call-done = bf16[4608,1152]{1,0:T(8,128)(2,1)} async-done(((bf16[288,1152]{1,0:T(8,128)(2,1)}), bf16[4608,1152]{1,0:T(8,128)(2,1)}) %all-gather.19.cloned.1.call-update) | async-done | bytes 10616848 | tf_op jit(solution)/shard_map/all_gather | solution.py:195
  309.7 8.6 fusion.93
  318.4 4.0 fusion.33
  323.2 7.9 fusion.19
  331.9 2.3 convolution_convert_fusion.3
  334.3 3.6 convolution_convert_fusion.4
  348.5 5.6 convolution_convert_fusion.2
  354.1 6.7 convolution_convert_fusion
  362.1 5.8 convolution_convert_fusion.1
  368.9 6.5 fusion.28
  378.5 9.4 all_to_all.29
  390.0 5.5 reduce-scatter.38.cloned.1.call-done
  397.5 100.0 %reduce-scatter.36.cloned.1.call-done = bf16[72,3456]{1,0:T(8,128)(2,1)} async-done(((bf16[1152,3456]{1,0:T(8,128)(2,1)}), bf16[72,3456]{1,0:T(8,128)(2,1)}) %reduce-scatter.36.cloned.1.call-update) | async-done | bytes 497680
  497.5 2.5 copy.107
  500.1 121.8 %reduce-scatter.26.cloned.1.call-done = bf16[288,1152]{1,0:T(8,128)(2,1)} async-done(((bf16[4608,1152]{1,0:T(8,128)(2,1)}), bf16[288,1152]{1,0:T(8,128)(2,1)}) %reduce-scatter.26.cloned.1.call-update) | async-done | bytes 663568 | tf_op jit(solution)/shard_map/reduce_scatter | solution.py:219
  621.9 2.6 copy.111
  624.7 121.7 %reduce-scatter.22.cloned.1.call-done = bf16[72,4608]{1,0:T(8,128)(2,1)} async-done(((bf16[1152,4608]{1,0:T(8,128)(2,1)}), bf16[72,4608]{1,0:T(8,128)(2,1)}) %reduce-scatter.22.cloned.1.call-update) | async-done | bytes 663568 | tf_op jit(solution)/shard_map/reduce_scatter | solution.py:216
  750.0 33.1 %reduce-scatter.34.cloned.1.call-done = f32[576,432]{1,0:T(8,128)} async-done(((f32[1152,432]{1,0:T(8,128)}), f32[576,432]{1,0:T(8,128)}) %reduce-scatter.34.cloned.1.call-update) | async-done | bytes 995344
  785.6 15.5 %reduce-scatter.30.cloned.1.call-done = f32[576,72]{1,0:T(8,128)} async-done(((f32[1152,72]{1,0:T(8,128)}), f32[576,72]{1,0:T(8,128)}) %reduce-scatter.30.cloned.1.call-update) | async-done | bytes 165904
  804.5 27.8 %reduce-scatter.28.cloned.1.call-done = f32[1728,72]{1,0:T(8,128)} async-done(((f32[3456,72]{1,0:T(8,128)}), f32[1728,72]{1,0:T(8,128)}) %reduce-scatter.28.cloned.1.call-update) | async-done | bytes 497680
  837.6 25.2 %reduce-scatter.32.cloned.1.call-done = f32[576,288]{1,0:T(8,128)} async-done(((f32[1152,288]{1,0:T(8,128)}), f32[576,288]{1,0:T(8,128)}) %reduce-scatter.32.cloned.1.call-update) | async-done | bytes 663568
  862.8 2.3 copy.112
  867.0 22.1 %reduce-scatter.24.cloned.1.call-done = f32[72,2304]{1,0:T(8,128)} async-done(((f32[72,4608]{1,0:T(8,128)}), f32[72,2304]{1,0:T(8,128)}) %reduce-scatter.24.cloned.1.call-update) | async-done | bytes 663568 | tf_op jit(solution)/shard_map/reduce_scatter | solution.py:226
  893.0 40.0 %all-reduce.3 = (f32[]{:T(128)}, f32[16128]{0:T(1024)S(1)}) all-reduce(f32[]{:T(128)S(6)} %add.349, f32[16128]{0:T(1024)S(1)} %constant_dynamic-update-slice_fusion.10), channel_id=1, replica_groups=mesh['rep'=2,'shard'=16] {'rep','shard'}, use_global_device_ids=true, to_apply=%region_32.33 | all-reduce | flops 16129 | bytes 129032 | tf_op jit(solution)/shard_map/psum | solution.py:232
  935.0 3.8 add_bitcast_fusion.1
  939.5 3.3 multiply_add_fusion.3
  942.9 2.4 fusion.27
  945.3 3.9 add_bitcast_fusion
  949.2 30.7 %all-reduce.6.cloned.1.call-done = f32[16,1152]{1,0:T(8,128)} async-done(((f32[16,1152]{1,0:T(8,128)}), f32[16,1152]{1,0:T(8,128)}) %all-reduce.6.cloned.1.call-update) | async-done | bytes 73744
  981.9 2.9 add_bitcast_fusion.2
  984.8 21.1 %all-gather.1 = f32[2,1728,72]{1,2,0:T(8,128)S(1)} all-gather(f32[1,1728,72]{1,2,0:T(8,128)S(1)} %get-tuple-element.56), channel_id=1, replica_groups=mesh['rep'=2,'shard'=16] {'rep'}, dimensions={0}, use_global_device_ids=true | all-gather | bytes 1492992 | tf_op jit(solution)/shard_map/all_gather | solution.py:252
  1009.2 9.2 all-gather.2
  1020.3 2.5 copy.100
  1024.8 19.7 %all-gather.21.cloned.1.call-done = f32[72,4608]{1,0:T(8,128)} async-done(((f32[72,2304]{1,0:T(8,128)}), f32[72,4608]{1,0:T(8,128)}) %all-gather.21.cloned.1.call-update) | async-done | bytes 1327120 | tf_op jit(solution)/shard_map/all_gather | solution.py:254
  1044.5 36.4 %all-gather.25.cloned.1.call-done = f32[2,576,432]{1,2,0:T(8,128)} async-done(((f32[1,576,432]{1,2,0:T(8,128)}), f32[2,576,432]{1,2,0:T(8,128)}) %all-gather.25.cloned.1.call-update) | async-done | bytes 1990672 | tf_op jit(solution)/shard_map/all_gather | solution.py:256
  1080.9 2.8 copy.101
  1083.6 2.4 reshape.469
  1086.0 2.5 copy.147
  (256 shorter events, 62.6 us)
Async XLA Ops:
  7.2 78.5 %all-gather.13.cloned.1.call-start = ((), (), s32[]{:S(2)}) async-start(), calls=%async_computation.11 | async-start | bytes 8460288 | tf_op jit(solution)/shard_map/all_gather | solution.py:190
  9.3 121.0 %all-gather.15.cloned.1.call-start = ((), (), s32[]{:S(2)}) async-start(), calls=%async_computation.12 | async-start | bytes 2820096 | tf_op jit(solution)/shard_map/all_gather | solution.py:191
  11.0 5.6 copy-start.60
  11.1 30.5 %copy-start.2 = (f32[1152,432]{0,1:T(8,128)S(1)}, f32[1152,432]{0,1:T(8,128)}, u32[]{:S(2)}) copy-start(f32[1152,432]{0,1:T(8,128)} %param.30) | copy-start | bytes 5971972
  11.1 209.3 %all-gather.17.cloned.1.call-start = ((), (), s32[]{:S(2)}) async-start(), calls=%async_computation.13 | async-start | bytes 11280384 | tf_op jit(solution)/shard_map/all_gather | solution.py:194
  13.5 32.8 %copy-start.1 = (bf16[1,128,1152]{2,1,0:T(8,128)(2,1)S(1)}, bf16[1,128,1152]{2,1,0:T(8,128)(2,1)}, u32[]{:S(2)}) copy-start(bf16[1,128,1152]{2,1,0:T(8,128)(2,1)} %param.22) | copy-start | bytes 884740
  13.5 33.2 %copy-start.18 = (f32[16128]{0:T(1024)S(1)}, f32[16128]{0:T(1024)}, u32[]{:S(2)}) copy-start(f32[16128]{0:T(1024)} %param.31) | copy-start | bytes 193540
  13.5 296.2 %all-gather.19.cloned.1.call-start = ((), (), s32[]{:S(2)}) async-start(), calls=%async_computation.14 | async-start | bytes 11280384 | tf_op jit(solution)/shard_map/all_gather | solution.py:195
  42.8 10.6 all-to-all-start
  46.3 349.2 %reduce-scatter.38.cloned.1.call-start = ((), (), s32[]{:S(2)}) async-start(), calls=%async_computation.27 | async-start | bytes 2820096
  46.5 43.9 %copy-start.41 = (f32[128]{0:T(128)}, f32[128]{0:T(128)S(1)}, u32[]{:S(2)}) copy-start(f32[128]{0:T(128)S(1)} %broadcast_multiply_fusion.5) | copy-start | bytes 1540
  47.3 43.1 %copy-start.49 = (f32[128]{0:T(128)}, f32[128]{0:T(128)S(1)}, u32[]{:S(2)}) copy-start(f32[128]{0:T(128)S(1)} %add_rsqrt_fusion.1) | copy-start | bytes 1540
  54.2 36.2 %copy-start.27 = (f32[1152]{0:T(1024)}, f32[1152]{0:T(1024)S(1)}, u32[]{:S(2)}) copy-start(f32[1152]{0:T(1024)S(1)} %get-tuple-element.36) | copy-start | bytes 13828
  54.2 76.1 %copy-start.32 = (f32[1152]{0:T(1024)}, f32[1152]{0:T(1024)S(1)}, u32[]{:S(2)}) copy-start(f32[1152]{0:T(1024)S(1)} %get-tuple-element.38) | copy-start | bytes 13828
  91.8 38.6 %copy-start.66 = (f32[16,128]{1,0:T(8,128)}, f32[16,128]{1,0:T(8,128)S(1)}, u32[]{:S(2)}) copy-start(f32[16,128]{1,0:T(8,128)S(1)} %get-tuple-element.79) | copy-start | bytes 24580
  91.8 41.8 %copy-start.64 = (f32[16,128,128]{1,2,0:T(8,128)}, f32[16,128,128]{1,2,0:T(8,128)S(1)}, u32[]{:S(2)}) copy-start(f32[16,128,128]{1,2,0:T(8,128)S(1)} %get-tuple-element.80) | copy-start | bytes 3145732
  133.6 86.9 %copy-start.46 = (f32[128]{0:T(128)}, f32[128]{0:T(128)S(1)}, u32[]{:S(2)}) copy-start(f32[128]{0:T(128)S(1)} %broadcast_multiply_fusion.4) | copy-start | bytes 1540
  309.7 8.6 copy-start
  309.7 8.6 copy-start.47
  309.7 8.6 copy-start.52
  334.2 163.3 %reduce-scatter.36.cloned.1.call-start = ((), (), s32[]{:S(2)}) async-start(), calls=%async_computation.26 | async-start | bytes 8460288
  354.1 267.9 %reduce-scatter.26.cloned.1.call-start = ((), (), s32[]{:S(2)}) async-start(), calls=%async_computation.17 | async-start | bytes 11280384 | tf_op jit(solution)/shard_map/reduce_scatter | solution.py:219
  360.9 385.5 %reduce-scatter.22.cloned.1.call-start = ((), (), s32[]{:S(2)}) async-start(), calls=%async_computation.15 | async-start | bytes 11280384 | tf_op jit(solution)/shard_map/reduce_scatter | solution.py:216
  367.9 9.0 copy-start.58
  367.9 9.0 copy-start.38
  367.9 9.0 copy-start.39
  367.9 9.1 copy-start.57
  367.9 20.1 %copy-start.25 = (bf16[16,1,1152]{2,1,0:T(2,128)(2,1)S(1)}, bf16[16,1,1152]{2,1,0:T(2,128)(2,1)}, u32[]{:S(2)}) copy-start(bf16[16,1,1152]{2,1,0:T(2,128)(2,1)} %copy-done.24) | copy-start | bytes 110596
  367.9 415.1 %reduce-scatter.34.cloned.1.call-start = ((), (), s32[]{:S(2)}) async-start(), calls=%async_computation.24 | async-start | bytes 3538944
  390.0 411.1 %reduce-scatter.30.cloned.1.call-start = ((), (), s32[]{:S(2)}) async-start(), calls=%async_computation.22 | async-start | bytes 884736
  397.5 434.8 %reduce-scatter.28.cloned.1.call-start = ((), (), s32[]{:S(2)}) async-start(), calls=%async_computation.21 | async-start | bytes 2654208
  500.1 362.7 %reduce-scatter.32.cloned.1.call-start = ((), (), s32[]{:S(2)}) async-start(), calls=%async_computation.23 | async-start | bytes 2654208
  624.5 124.2 %copy-start.37 = (f32[16,72]{1,0:T(8,128)S(1)}, f32[16,72]{1,0:T(8,128)}, u32[]{:S(2)}) copy-start(f32[16,72]{1,0:T(8,128)} %get-tuple-element.73) | copy-start | bytes 13828
  624.5 124.3 %copy-start.56 = (f32[16,72]{1,0:T(8,128)S(1)}, f32[16,72]{1,0:T(8,128)}, u32[]{:S(2)}) copy-start(f32[16,72]{1,0:T(8,128)} %get-tuple-element.71) | copy-start | bytes 13828
  624.6 124.4 %copy-start.55 = (f32[1152]{0:T(1024)S(1)}, f32[1152]{0:T(1024)}, u32[]{:S(2)}) copy-start(f32[1152]{0:T(1024)} %get-tuple-element.69) | copy-start | bytes 13828
  624.6 124.5 %copy-start.40 = (f32[4608]{0:T(1024)S(1)}, f32[4608]{0:T(1024)}, u32[]{:S(2)}) copy-start(f32[4608]{0:T(1024)} %get-tuple-element.86) | copy-start | bytes 55300
  624.6 124.5 %copy-start.54 = (f32[1152]{0:T(1024)S(1)}, f32[1152]{0:T(1024)}, u32[]{:S(2)}) copy-start(f32[1152]{0:T(1024)} %get-tuple-element.31) | copy-start | bytes 13828
  624.6 124.5 %copy-start.3 = (f32[1152,432]{0,1:T(8,128)S(1)}, f32[1152,432]{0,1:T(8,128)}, u32[]{:S(2)}) copy-start(f32[1152,432]{0,1:T(8,128)} %param.30) | copy-start | bytes 5971972
  624.6 264.5 %reduce-scatter.24.cloned.1.call-start = ((), (), s32[]{:S(2)}) async-start(), calls=%async_computation.16 | async-start | bytes 1990656 | tf_op jit(solution)/shard_map/reduce_scatter | solution.py:226
  748.6 231.3 %all-reduce.6.cloned.1.call-start = ((), (), s32[]{:S(2)}) async-start(), calls=%async_computation.25 | async-start | bytes 147456
  892.9 127.4 %all-gather.23.cloned.1.call-start = ((), (), s32[]{:S(2)}) async-start(), calls=%async_computation.19 | async-start | bytes 2211840 | tf_op jit(solution)/shard_map/all_gather | solution.py:255
  938.8 105.7 %all-gather.21.cloned.1.call-start = ((), (), s32[]{:S(2)}) async-start(), calls=%async_computation.18 | async-start | bytes 1990656 | tf_op jit(solution)/shard_map/all_gather | solution.py:254
  942.8 138.1 %all-gather.25.cloned.1.call-start = ((), (), s32[]{:S(2)}) async-start(), calls=%async_computation.20 | async-start | bytes 3317760 | tf_op jit(solution)/shard_map/all_gather | solution.py:256
  945.3 34.6 %copy-start.44 = (f32[1,1152]{1,0:T(1,128)S(1)}, f32[1,1152]{1,0:T(1,128)}, u32[]{:S(2)}) copy-start(f32[1,1152]{1,0:T(1,128)} %get-tuple-element.63) | copy-start | bytes 13828
  945.3 34.6 %copy-start.45 = (f32[1,1152]{1,0:T(1,128)S(1)}, f32[1,1152]{1,0:T(1,128)}, u32[]{:S(2)}) copy-start(f32[1,1152]{1,0:T(1,128)} %get-tuple-element.64) | copy-start | bytes 13828
  1006.5 13.1 %copy-start.19 = (f32[16128]{0:T(1024)S(1)}, f32[16128]{0:T(1024)}, u32[]{:S(2)}) copy-start(f32[16128]{0:T(1024)} %param.31) | copy-start | bytes 193540
  1006.5 13.1 %copy-start.34 = (f32[16128]{0:T(1024)S(1)}, f32[16128]{0:T(1024)}, u32[]{:S(2)}) copy-start(f32[16128]{0:T(1024)} %param.37) | copy-start | bytes 193540
  1006.5 13.1 %copy-start.35 = (f32[16128]{0:T(1024)S(1)}, f32[16128]{0:T(1024)}, u32[]{:S(2)}) copy-start(f32[16128]{0:T(1024)} %param.43) | copy-start | bytes 193540
  (38 other events, 92.1 us)
Sparse Core Ops, SparseCore 0:
  10.7 74.9 all-gather.12
  88.5 41.8 all-gather.14
  133.2 87.1 all-gather.16
  223.1 86.5 all-gather.18
  334.3 61.1 reduce-scatter.37
  399.5 97.9 reduce-scatter.35
  501.6 120.3 reduce-scatter.25
  626.0 120.2 reduce-scatter.21
  748.6 34.3 reduce-scatter.33
  785.7 15.3 reduce-scatter.29
  804.0 28.3 reduce-scatter.27
  834.4 28.3 reduce-scatter.31
  865.6 23.4 reduce-scatter.23
  893.0 86.8 all-reduce.5
  981.9 35.6 all-gather.22
  1019.6 24.8 all-gather.20
  1046.5 34.3 all-gather.24
where the time goes:
time: 1110 us; the launch traced here: 1100 us
  waiting for transfers between devices  804 us (72%)
  blocking collectives  104 us (9%)
  matrix products  73.5 us (7%)
  other arithmetic  45.3 us (4%)
  local copies, waits for them, and re-layouts  43.6 us (4%)
  between operations  20.5 us (2%)
    unnamed x24, waiting for transfers between devices  238 us
    reduce_scatter x1, waiting for transfers between devices, shards(): lax.psum_scatter(grads[3].astype(jnp.bfloat16), 'shard', scatter_dimensio...  122 us
    reduce_scatter x1, waiting for transfers between devices, shards(): lax.psum_scatter(grads[2].astype(jnp.bfloat16), 'shard', scatter_dimensio...  122 us
    all_gather x1, waiting for transfers between devices, shards(): lax.all_gather(w_fc1.astype(jnp.bfloat16), 'shard', axis=0, tiled=True)  86.1 us
    all_gather x1, waiting for transfers between devices, shards(): lax.all_gather(w_fc2.astype(jnp.bfloat16), 'shard', axis=0, tiled=True)  83.5 us
    dot_general x17, matrix products, product(): return jnp.einsum(form, left, right, preferred_element_type=jnp.float32)  69.8 us
    psum x1, blocking collectives, shards(): lax.psum((bias_partial, weight_squares), ('rep', 'shard'))  40 us
    all_gather x1, waiting for transfers between devices, shards(): lax.all_gather(w_proj.astype(jnp.bfloat16), 'shard', axis=0, tiled=True)  38.2 us
  transfers between devices with their start and end apart: 18, of which 17 were waited for; matrix products, arithmetic and copies ran while one was open for 11% of the time, Pallas kernels for 0%

commit v1 on v0

v1 whole, which is shorter than its diff:
```python
import math

import jax
import jax.numpy as jnp
from jax import lax
from jax.sharding import PartitionSpec as P

HD = 72
H = 16
FF = 4608


ln_eps = 1e-06
beta_one = 0.9
beta_two = 0.999
adam_eps = 1e-08
learn_rate = 0.03
decay_rate = 0.01
step_count = 2
gelu_coef = 0.044715


def product(form, left, right):
    return jnp.einsum(form, left, right, preferred_element_type=jnp.float32)


def normalize(rows):
    center = rows - jnp.mean(rows, axis=-1, keepdims=True)
    rstd = lax.rsqrt(jnp.mean(center * center, axis=-1, keepdims=True) + ln_eps)
    return (center * rstd, rstd)


def norm_back(grad, normed, rstd):
    return rstd * (
        grad
        - jnp.mean(grad, axis=-1, keepdims=True)
        - normed * jnp.mean(grad * normed, axis=-1, keepdims=True)
    )


def gelu_parts(pre):
    root = math.sqrt(2.0 / math.pi)
    inner = root * (pre + gelu_coef * pre * pre * pre)
    tangent = jnp.tanh(inner)
    value = 0.5 * pre * (1.0 + tangent)
    slope = 0.5 * (1.0 + tangent) + 0.5 * pre * (1.0 - tangent * tangent) * root * (
        1.0 + 3.0 * gelu_coef * pre * pre
    )
    return (value, slope)


def time_embed(steps, width):
    half = width // 2
    freqs = jnp.exp(-math.log(10000.0) * jnp.arange(half, dtype=jnp.float32) / half)
    angles = steps.astype(jnp.float32)[:, None] * freqs[None, :]
    return jnp.concatenate([jnp.cos(angles), jnp.sin(angles)], axis=1)


def adam_change(weight, grad, first, second, clip):
    scaled = grad * clip
    first_new = beta_one * first + (1.0 - beta_one) * scaled
    second_new = beta_two * second + (1.0 - beta_two) * scaled * scaled
    first_hat = first_new / (1.0 - beta_one**step_count)
    second_hat = second_new / (1.0 - beta_two**step_count)
    change = -learn_rate * (first_hat / (jnp.sqrt(second_hat) + adam_eps) + decay_rate * weight)
    return (change, first_new, second_new)


def shards(
    latents,
    cond,
    timesteps,
    cotangent,
    w_qkv,
    w_proj,
    w_fc1,
    w_fc2,
    w_ada,
    biases,
    m_qkv,
    m_proj,
    m_fc1,
    m_fc2,
    m_ada,
    m_bias,
    v_qkv,
    v_proj,
    v_fc1,
    v_fc2,
    v_ada,
    v_bias,
):
    axes = ("rep", "shard")
    replicas = lax.axis_size("rep")
    parts = lax.axis_size("shard")
    devices = replicas * parts
    rank = lax.axis_index("rep")
    turn = rank % 2
    couples = [(i, i ^ 1) for i in range(replicas)]
    length, width = latents.shape[1:]
    inner = H * HD
    half = inner // 2
    heads = H // 2
    rows = w_qkv.shape[0]
    folds = FF // (2 * width)
    unit = FF // (2 * parts * folds)

    def swap(value):
        return lax.ppermute(value, "rep", couples)

    def ordered(own, other, axis):
        first = jnp.concatenate([own, other], axis=axis)
        second = jnp.concatenate([other, own], axis=axis)
        return jnp.where(turn == 0, first, second)

    def own_half(value, axis):
        count = value.shape[axis] // 2
        return lax.dynamic_slice_in_dim(value, turn * count, count, axis)

    def spread(value):
        copies = jnp.broadcast_to(value, (devices,) + value.shape[1:])
        return lax.all_to_all(copies, axes, split_axis=0, concat_axis=0, tiled=True)

    b_q = own_half(biases[0:inner], 0)
    b_v = own_half(biases[inner : 2 * inner], 0)
    b_proj = biases[2 * inner : 2 * inner + width]
    b_fc1 = biases[2 * inner + width : 2 * inner + width + FF]
    b_fc2 = biases[2 * inner + width + FF : 2 * inner + 2 * width + FF]
    b_ada = biases[biases.shape[0] - 6 * width :]
    units = lax.dynamic_index_in_dim(
        b_fc1.reshape(parts, 2, folds, unit), turn, 1, keepdims=False
    )
    b_one = jnp.transpose(units, (1, 0, 2)).reshape(folds, width)

    wq_half = own_half(w_qkv.astype(jnp.bfloat16).reshape(rows, 3, inner), 2)
    pack_attn = jnp.concatenate(
        [w_proj.astype(jnp.bfloat16), wq_half.reshape(rows, 3 * half)], axis=1
    )
    full_attn = lax.all_gather(pack_attn, "shard", axis=0, tiled=True)
    wp_b = full_attn[:, :width]
    wq_b = full_attn[:, width:]
    w1_half = lax.dynamic_index_in_dim(
        w_fc1.astype(jnp.bfloat16).reshape(rows, parts, 2, folds, unit), turn, 2, keepdims=False
    )
    w1_half = jnp.transpose(w1_half, (0, 2, 1, 3)).reshape(rows, folds * width)
    w2_half = own_half(w_fc2.astype(jnp.bfloat16), 0).reshape(folds, rows, width)
    pack_mlp = jnp.concatenate([w1_half] + [w2_half[f] for f in range(folds)], axis=1)
    full_mlp = lax.all_gather(pack_mlp, "shard", axis=0, tiled=True)
    w1_b = [full_mlp[:, f * width : (f + 1) * width] for f in range(folds)]
    w2_b = [full_mlp[:, (folds + f) * width : (folds + f + 1) * width] for f in range(folds)]

    cvec = cond + time_embed(timesteps, width)
    silu_c = jax.nn.silu(cvec).astype(jnp.bfloat16)
    ada_local = w_ada.astype(jnp.bfloat16)
    silu_all = spread(silu_c)
    silu_group = lax.dynamic_slice_in_dim(silu_all, rank * parts, parts, 0)
    mod_cols = jnp.dot(silu_group, ada_local, preferred_element_type=jnp.float32)
    mod = lax.all_to_all(mod_cols, "shard", split_axis=0, concat_axis=1, tiled=True) + b_ada
    shift1, scale1, gate1, shift2, scale2, gate2 = [
        mod[:, i * width : (i + 1) * width] for i in range(6)
    ]

    tokens = latents[0].astype(jnp.float32)
    n_one, r_one = normalize(tokens)
    a_one = (n_one * (1.0 + scale1) + shift1).astype(jnp.bfloat16)
    grad_out = cotangent[0].astype(jnp.float32)
    d_mlp = grad_out * gate2
    d_mlp_b = d_mlp.astype(jnp.bfloat16)
    a_one2 = jnp.concatenate([a_one, swap(a_one)], axis=0)
    d_mlp2 = jnp.concatenate([d_mlp_b, swap(d_mlp_b)], axis=0)

    qkv = product("ld,de->le", a_one2, wq_b)
    shape = (2, length, heads, HD)
    queries = (qkv[:, :half] + b_q).astype(jnp.bfloat16).reshape(shape)
    key_rows = qkv[:, half : 2 * half].astype(jnp.bfloat16).reshape(shape)
    value_rows = (qkv[:, 2 * half :] + b_v).astype(jnp.bfloat16).reshape(shape)
    factor = HD ** (-0.5)
    scores = product("bqhd,bkhd->bhqk", queries, key_rows) * factor
    top = jnp.max(scores, axis=-1, keepdims=True)
    expo = jnp.exp(scores - top)
    probs = expo / jnp.sum(expo, axis=-1, keepdims=True)
    probs_b = probs.astype(jnp.bfloat16)
    heads_out = product("bhqk,bkhd->bqhd", probs_b, value_rows).astype(jnp.bfloat16)
    heads_flat = heads_out.reshape(2, length, half)
    heads_other = swap(heads_flat)[::-1]
    heads_own = ordered(heads_flat[0], heads_other[0], 1)
    attn = product("le,ed->ld", heads_own, wp_b) + b_proj
    x_one = tokens + gate1 * attn
    n_two, r_two = normalize(x_one)
    a_two = (n_two * (1.0 + scale2) + shift2).astype(jnp.bfloat16)
    a_two2 = jnp.concatenate([a_two, swap(a_two)], axis=0)

    mlp_sum = 0.0
    d_a2_sum = 0.0
    g_one = []
    g_two = []
    g_b_one = []
    for f in range(folds):
        pre = product("ld,df->lf", a_two2, w1_b[f]) + b_one[f]
        act_val, act_slope = gelu_parts(pre)
        act = act_val.astype(jnp.bfloat16)
        mlp_sum = mlp_sum + product("lf,fd->ld", act, w2_b[f])
        d_pre = product("ld,fd->lf", d_mlp2, w2_b[f]) * act_slope
        d_pre_b = d_pre.astype(jnp.bfloat16)
        d_a2_sum = d_a2_sum + product("lf,df->ld", d_pre_b, w1_b[f])
        g_one.append(product("ld,lf->df", a_two2, d_pre_b).astype(jnp.bfloat16))
        g_two.append(product("lf,ld->fd", act, d_mlp2).astype(jnp.bfloat16))
        g_b_one.append(jnp.sum(d_pre, axis=0))
    grads_mlp = lax.psum_scatter(
        jnp.concatenate(g_one + g_two, axis=1), "shard", scatter_dimension=0, tiled=True
    )
    d_a2 = d_a2_sum[:length] + swap(d_a2_sum[length:].astype(jnp.bfloat16)).astype(jnp.float32)
    mlp = (
        mlp_sum[:length]
        + swap(mlp_sum[length:].astype(jnp.bfloat16)).astype(jnp.float32)
        + b_fc2
    )
    block_out = (x_one + gate2 * mlp)[None]
    d_gate2 = jnp.sum(grad_out * mlp, axis=0)
    g_b_fc2 = jnp.sum(d_mlp, axis=0)

    d_shift2 = jnp.sum(d_a2, axis=0)
    d_scale2 = jnp.sum(d_a2 * n_two, axis=0)
    dx_one = grad_out + norm_back(d_a2 * (1.0 + scale2), n_two, r_two)
    d_gate1 = jnp.sum(dx_one * attn, axis=0)
    d_attn = dx_one * gate1
    d_attn_b = d_attn.astype(jnp.bfloat16)
    g_b_proj = jnp.sum(d_attn, axis=0)
    d_attn2 = jnp.concatenate([d_attn_b, swap(d_attn_b)], axis=0)
    d_heads = (
        product("ld,ed->le", d_attn2, own_half(wp_b, 0)).astype(jnp.bfloat16).reshape(shape)
    )
    heads_all = jnp.concatenate(
        [heads_own, ordered(heads_flat[1], heads_other[1], 1)], axis=0
    )
    g_proj = product("le,ld->ed", heads_all, own_half(d_attn2, 1)).astype(jnp.bfloat16)
    delta = jnp.sum(d_heads.astype(jnp.float32) * heads_out.astype(jnp.float32), axis=-1)
    delta = jnp.transpose(delta, (0, 2, 1))[..., None]
    d_probs = product("bqhd,bkhd->bhqk", d_heads, value_rows)
    d_scores = (probs * (d_probs - delta) * factor).astype(jnp.bfloat16)
    d_q = product("bhqk,bkhd->bqhd", d_scores, key_rows)
    d_k = product("bhqk,bqhd->bkhd", d_scores, queries)
    d_v = product("bhqk,bqhd->bkhd", probs_b, d_heads)
    g_b_q = jnp.sum(d_q, axis=(0, 1)).reshape(half)
    g_b_v = jnp.sum(d_v, axis=(0, 1)).reshape(half)
    d_qkv = jnp.concatenate(
        [piece.astype(jnp.bfloat16).reshape(2 * length, half) for piece in (d_q, d_k, d_v)],
        axis=1,
    )
    g_qkv = product("ld,le->de", a_one2, d_qkv).astype(jnp.bfloat16)
    grads_attn = lax.psum_scatter(
        jnp.concatenate([g_proj, g_qkv], axis=1), "shard", scatter_dimension=0, tiled=True
    )
    d_a1_sum = product("le,de->ld", d_qkv, wq_b)
    d_a1 = d_a1_sum[:length] + swap(d_a1_sum[length:].astype(jnp.bfloat16)).astype(jnp.float32)
    d_shift1 = jnp.sum(d_a1, axis=0)
    d_scale1 = jnp.sum(d_a1 * n_one, axis=0)
    latents_grad = (dx_one + norm_back(d_a1 * (1.0 + scale1), n_one, r_one))[None]

    d_mod = jnp.concatenate([d_shift1, d_scale1, d_gate1, d_shift2, d_scale2, d_gate2])
    d_mod_b = d_mod.astype(jnp.bfloat16).reshape(1, parts, d_mod.shape[0] // parts)
    d_mod_b = jnp.broadcast_to(d_mod_b, (replicas,) + d_mod_b.shape[1:])
    d_mod_cols = lax.all_to_all(
        d_mod_b.reshape(devices, d_mod_b.shape[2]), axes, split_axis=0, concat_axis=0, tiled=True
    )
    g_ada = jnp.dot(silu_all.T, d_mod_cols, preferred_element_type=jnp.float32)
    group_cols = lax.dynamic_slice_in_dim(d_mod_cols, rank * parts, parts, 0)
    silu_terms = jnp.dot(group_cols, ada_local.T, preferred_element_type=jnp.float32)
    silu_terms = lax.all_to_all(silu_terms, "shard", split_axis=0, concat_axis=0, tiled=True)
    silu_grad = jnp.sum(silu_terms, axis=0, keepdims=True)
    sig = jax.nn.sigmoid(cvec)
    cond_grad = silu_grad * sig * (1.0 + cvec * (1.0 - sig))

    mine = jnp.arange(2) == turn
    units_one = jnp.transpose(jnp.stack(g_b_one).reshape(folds, parts, unit), (1, 0, 2))
    bias_partial = jnp.concatenate(
        [
            jnp.where(mine[:, None], g_b_q[None], 0.0).reshape(inner),
            jnp.where(mine[:, None], g_b_v[None], 0.0).reshape(inner),
            g_b_proj,
            jnp.where(mine[None, :, None, None], units_one[:, None], 0.0).reshape(FF),
            g_b_fc2,
            d_mod,
        ]
    )
    chunk = bias_partial.shape[0] // devices
    bias_terms = lax.all_to_all(
        bias_partial.reshape(devices, chunk), axes, split_axis=0, concat_axis=0, tiled=True
    )
    bias_chunk = jnp.sum(bias_terms, axis=0)

    def complete(own):
        return swap(own) if replicas == 2 else jnp.zeros_like(own)

    def share(own, axis):
        if replicas == 2:
            return own
        return lax.psum_scatter(
            own.astype(jnp.float32), "rep", scatter_dimension=axis, tiled=True
        )

    def split(value):
        if replicas == 2:
            return own_half(value, 1)
        return share(value, 1)

    own_proj = grads_attn[:, :half]
    if replicas > 2:
        own_proj = share(ordered(own_proj, jnp.zeros_like(own_proj), 1), 1)
    own_qkv = grads_attn[:, half:].reshape(rows, 3, half)
    full_qkv = ordered(own_qkv, complete(own_qkv), 2).reshape(rows, 3 * inner)
    own_mlp = grads_mlp[:, None]
    full_mlp_grad = ordered(own_mlp, complete(own_mlp), 1)
    full_one = full_mlp_grad[:, :, : folds * width].reshape(rows, 2, folds, parts, unit)
    full_one = jnp.transpose(full_one, (0, 3, 1, 2, 4)).reshape(rows, FF)
    full_two = full_mlp_grad[:, :, folds * width :].reshape(rows, 2, folds, width)
    full_two = jnp.transpose(full_two, (1, 2, 0, 3)).reshape(2 * folds * rows, width)
    count_ada = width // replicas
    own_ada = lax.dynamic_slice_in_dim(g_ada, rank * count_ada, count_ada, 0)
    pieces = [split(full_qkv), own_proj, split(full_one), split(full_two), own_ada]
    pieces = [piece.astype(jnp.float32) for piece in pieces]
    if replicas == 2:
        counted = [grads_attn.astype(jnp.float32), grads_mlp.astype(jnp.float32), own_ada]
    else:
        counted = pieces
    squares = sum((jnp.sum(p * p) for p in counted)) + jnp.sum(bias_chunk * bias_chunk)
    totals = spread(jnp.concatenate([bias_chunk, squares[None]])[None])
    g_bias = totals[:, :chunk].reshape(devices * chunk)
    gnorm = jnp.sqrt(jnp.sum(totals[:, chunk]))
    clip = 1.0 / jnp.maximum(gnorm, 1.0)

    weights = (w_qkv, w_proj, w_fc1, w_fc2, w_ada)
    dims = (1, 1, 1, 1, 0)
    firsts = (m_qkv, m_proj, m_fc1, m_fc2, m_ada)
    seconds = (v_qkv, v_proj, v_fc1, v_fc2, v_ada)
    new_w = []
    new_m = []
    new_v = []
    for weight, dim, grad, first, second in zip(weights, dims, pieces, firsts, seconds):
        count = weight.shape[dim] // replicas
        own = lax.dynamic_slice_in_dim(weight, rank * count, count, dim)
        change, first_new, second_new = adam_change(own, grad, first, second, clip)
        change = change.astype(jnp.bfloat16)
        if replicas == 2:
            changes = ordered(change, swap(change), dim)
        else:
            changes = lax.all_gather(change, "rep", axis=dim, tiled=True)
        new_w.append(weight + changes.astype(jnp.float32))
        new_m.append(first_new)
        new_v.append(second_new)
    bias_update, new_m_bias, new_v_bias = adam_change(biases, g_bias, m_bias, v_bias, clip)
    return (
        block_out,
        latents_grad,
        cond_grad,
        *new_w,
        bias_update,
        *new_m,
        new_m_bias,
        *new_v,
        new_v_bias,
    )


def solution(mesh):
    in_specs = (
        P(("rep", "shard"), None, None),
        P(("rep", "shard"), None),
        P(("rep", "shard")),
        P(("rep", "shard"), None, None),
        P("shard", None),
        P("shard", None),
        P("shard", None),
        P("shard", None),
        P(None, "shard"),
        P(),
        P("shard", "rep"),
        P("shard", "rep"),
        P("shard", "rep"),
        P("shard", "rep"),
        P("rep", "shard"),
        P(),
        P("shard", "rep"),
        P("shard", "rep"),
        P("shard", "rep"),
        P("shard", "rep"),
        P("rep", "shard"),
        P(),
    )
    out_specs = (
        P(("rep", "shard"), None, None),
        P(("rep", "shard"), None, None),
        P(("rep", "shard"), None),
        P("shard", None),
        P("shard", None),
        P("shard", None),
        P("shard", None),
        P(None, "shard"),
        P(),
        P("shard", "rep"),
        P("shard", "rep"),
        P("shard", "rep"),
        P("shard", "rep"),
        P("rep", "shard"),
        P(),
        P("shard", "rep"),
        P("shard", "rep"),
        P("shard", "rep"),
        P("shard", "rep"),
        P("rep", "shard"),
        P(),
    )
    return jax.shard_map(shards, mesh=mesh, in_specs=in_specs, out_specs=out_specs, check_vma=False)
```

time: 1110 us -> 533 us (0.48)
  waiting for transfers between devices: 804 us -> 244 us
  blocking collectives: 104 us -> 0 us
  other arithmetic: 45.3 us -> 88.4 us
  local copies, waits for them, and re-layouts: 43.6 us -> 84.7 us
  starting transfers between devices: 4.42 us -> 41.5 us
  matrix products: 73.5 us -> 46.5 us
    reduce_scatter x3 -> x0, waiting for transfers between devices: 266 us -> none  [the longest x1 122 us: shards(): lax.psum_scatter(grads[3].astype(jnp.bfloat16), 'shard', scatter_dimensio...]
    all_gather x7 -> x2, waiting for transfers between devices: 295 us -> 80 us  [the longest x1 58.5 us: shards(): full_mlp = lax.all_gather(pack_mlp, 'shard', axis=0, tiled=True)]
    unnamed x24 -> x6, waiting for transfers between devices: 238 us -> 87.4 us
    all_gather x3 -> x0, blocking collectives: 54.4 us -> none  [the longest x1 24.2 us: shards(): silu_group = lax.all_gather(silu_c, 'shard', axis=0, tiled=True)]
    ppermute x0 -> x15, waiting for transfers between devices: none -> 46.9 us  [swap(): return lax.ppermute(value, 'rep', couples)]
    psum x1 -> x0, blocking collectives: 40 us -> none  [shards(): lax.psum((bias_partial, weight_squares), ('rep', 'shard'))]
    concatenate x1 -> x6, other arithmetic: 0.07 us -> 32.6 us  [the longest x1 28.2 us: shards(): jnp.concatenate(g_one + g_two, axis=1)]
    dot_general x17 -> x23, matrix products: 69.8 us -> 44 us  [product(): return jnp.einsum(form, left, right, preferred_element_type=jnp.float32)]
  transfers between devices with their start and end apart: 18 -> 25, of which waited for: 17 -> 17; matrix products, arithmetic and copies ran while one was open for 11% -> 34% of each run, Pallas kernels for 0% -> 0%
where the time goes in v1:
time: 533 us; the launch traced here: 525 us
  waiting for transfers between devices  244 us (46%)
  other arithmetic  88.4 us (17%)
  local copies, waits for them, and re-layouts  84.7 us (16%)
  matrix products  46.5 us (9%)
  starting transfers between devices  41.5 us (8%)
  between operations  19.5 us (4%)
    unnamed x6, waiting for transfers between devices  87.4 us
    all_gather x1, waiting for transfers between devices, shards(): full_mlp = lax.all_gather(pack_mlp, 'shard', axis=0, tiled=True)  58.5 us
    unnamed x164, local copies, waits for them, and re-layouts  54.4 us
    ppermute x15, waiting for transfers between devices, swap(): return lax.ppermute(value, 'rep', couples)  46.9 us
    dot_general x23, matrix products, product(): return jnp.einsum(form, left, right, preferred_element_type=jnp.float32)  44 us
    concatenate x1, other arithmetic, shards(): jnp.concatenate(g_one + g_two, axis=1)  28.2 us
    all_gather x1, waiting for transfers between devices, shards(): full_attn = lax.all_gather(pack_attn, 'shard', axis=0, tiled=True)  21.5 us
    ppermute x15, starting transfers between devices, swap(): return lax.ppermute(value, 'rep', couples)  16.9 us
  transfers between devices with their start and end apart: 25, of which 17 were waited for; matrix products, arithmetic and copies ran while one was open for 34% of the time, Pallas kernels for 0%

profile of v1, /device:TPU:0, one launch (start us, length us, event | category | flops | bytes accessed | tf_op | source)
XLA Modules:
  0.0 525.0 jit_solution(11382499632518451920)
XLA Ops:
  10.5 2.6 reshape.278
  20.7 7.3 %all-to-all-start = ((bf16[32,2,576]{2,1,0:T(2,128)(2,1)}), bf16[32,2,576]{2,1,0:T(2,128)(2,1)S(1)}, u32[]{:S(2)}, u32[]{:S(2)}) async-start(bf16[32,2,576]{2,1,0:T(2,128)(2,1)} %reshape.315), calls=%async_computation | async-start | bytes 163840 | tf_op jit(solution)/shard_map/all_to_all | solution.py:122
  28.5 8.4 %all-to-all-done = bf16[32,2,576]{2,1,0:T(2,128)(2,1)S(1)} async-done(((bf16[32,2,576]{2,1,0:T(2,128)(2,1)}), bf16[32,2,576]{2,1,0:T(2,128)(2,1)S(1)}, u32[]{:S(2)}, u32[]{:S(2)}) %all-to-all-start) | async-done | bytes 73760 | tf_op jit(solution)/shard_map/all_to_all | solution.py:122
  38.2 3.7 all-to-all-start.1
  42.3 6.2 %all-to-all-done.1 = f32[16,1,432]{2,1,0:T(1,128)S(1)} async-done(((f32[16,1,432]{2,1,0:T(1,128)}), f32[16,1,432]{2,1,0:T(1,128)S(1)}, u32[]{:S(2)}, u32[]{:S(2)}) %all-to-all-start.1) | async-done | bytes 27680 | tf_op jit(solution)/shard_map/all_to_all | solution.py:158
  50.1 7.9 %collective-permute-done = bf16[128,1152]{1,0:T(8,128)(2,1)S(1)} collective-permute-done((bf16[128,1152]{1,0:T(8,128)(2,1)S(1)}, bf16[128,1152]{1,0:T(8,128)(2,1)S(1)}, u32[]{:S(2)}, u32[]{:S(2)}) %collective-permute-start) | collective-permute-done | bytes 294944 | tf_op jit(solution)/shard_map/ppermute | solution.py:109
  57.9 21.5 %all-gather.3.cloned.1.call-done = bf16[1152,2880]{1,0:T(8,128)(2,1)} async-done(((bf16[72,2880]{1,0:T(8,128)(2,1)}), bf16[1152,2880]{1,0:T(8,128)(2,1)}) %all-gather.3.cloned.1.call-update) | async-done | bytes 6635536 | tf_op jit(solution)/shard_map/all_gather | solution.py:139
  79.4 4.0 fusion.3
  89.5 6.8 %collective-permute-done.1 = bf16[2,128,576]{1,2,0:T(8,128)(2,1)S(1)} collective-permute-done((bf16[2,128,576]{1,2,0:T(8,128)(2,1)S(1)}, bf16[2,128,576]{1,2,0:T(8,128)(2,1)S(1)}, u32[]{:S(2)}, u32[]{:S(2)}) %collective-permute-start.1) | collective-permute-done | bytes 294944 | tf_op jit(solution)/shard_map/ppermute | solution.py:109
  97.1 3.3 fusion.121
  103.7 7.1 %collective-permute-done.2 = bf16[128,1152]{1,0:T(8,128)(2,1)S(1)} collective-permute-done((bf16[128,1152]{1,0:T(8,128)(2,1)S(1)}, bf16[128,1152]{1,0:T(8,128)(2,1)S(1)}, u32[]{:S(2)}, u32[]{:S(2)}) %collective-permute-start.2) | collective-permute-done | bytes 294944 | tf_op jit(solution)/shard_map/ppermute | solution.py:109
  110.8 58.5 %all-gather.5.cloned.1.call-done = bf16[1152,4608]{1,0:T(8,128)(2,1)} async-done(((bf16[72,4608]{1,0:T(8,128)(2,1)}), bf16[1152,4608]{1,0:T(8,128)(2,1)}) %all-gather.5.cloned.1.call-update) | async-done | bytes 10616848 | tf_op jit(solution)/shard_map/all_gather | solution.py:148
  169.3 2.9 convolution_add_fusion.3
  172.3 3.9 convolution_add_fusion.2
  176.2 2.7 fusion.135
  180.7 2.8 fusion.134
  189.4 5.2 collective-permute-done.5
  195.4 4.7 collective-permute-done.3
  204.6 6.0 %collective-permute-done.6 = bf16[128,1152]{1,0:T(8,128)(2,1)S(1)} collective-permute-done((bf16[128,1152]{1,0:T(8,128)(2,1)S(1)}, bf16[128,1152]{1,0:T(8,128)(2,1)S(1)}, u32[]{:S(2)}, u32[]{:S(2)}) %collective-permute-start.6) | collective-permute-done | bytes 294944 | tf_op jit(solution)/shard_map/ppermute | solution.py:109
  221.4 2.7 pad_maximum_fusion.1
  224.1 8.6 %copy.290 = bf16[1152,2304]{1,0:T(8,128)(2,1)} copy(bf16[1152,2304]{0,1:T(8,128)(2,1)} %pad_maximum_fusion.1) | data formatting | bytes 10616832
  237.1 2.3 convolution_convert_fusion
  239.5 2.2 convolution_convert_fusion.1
  241.7 28.2 %pad_maximum_fusion = bf16[1152,4608]{0,1:T(8,128)(2,1)} fusion(bf16[1152,1152]{0,1:T(8,128)(2,1)S(1)} %convolution_convert_fusion, bf16[1152,1152]{0,1:T(8,128)(2,1)S(1)} %convolution_convert_fusion.1, bf16[1152,1152]{0,1:T(8,128)(2,1)S(1)} %convolution_convert_fusion.2, bf16[1152,1152]{0,1:T(8,128)(2,1)S(1)} %convolution_convert_fusion.3), kind=kLoop, calls=%fused_computation.1 | loop fusion | flops 42467328 | bytes 21233664 | tf_op jit(solution)/shard_map/concatenate | solution.py:210
  269.8 15.4 %copy.292 = bf16[1152,4608]{1,0:T(8,128)(2,1)} copy(bf16[1152,4608]{0,1:T(8,128)(2,1)} %pad_maximum_fusion) | data formatting | bytes 21233664
  290.6 4.0 fusion.1
  311.0 2.6 all-to-all-start.2
  313.6 2.2 fusion.55
  316.6 4.3 all-to-all-done.2
  320.8 2.6 all-to-all-start.4
  324.5 6.3 %all-to-all-done.4 = f32[32,1,504]{2,1,0:T(1,128)S(1)} async-done(((f32[32,1,504]{2,1,0:T(1,128)}), f32[32,1,504]{2,1,0:T(1,128)S(1)}, u32[]{:S(2)}, u32[]{:S(2)}) %all-to-all-start.4) | async-done | bytes 64544 | tf_op jit(solution)/shard_map/all_to_all | solution.py:287
  330.8 3.5 all-to-all-start.3
  337.7 3.5 all-to-all-done.3
  345.3 87.4 %reduce-scatter.9.cloned.1.call-done = bf16[72,4608]{1,0:T(8,128)(2,1)} async-done(((bf16[1152,4608]{1,0:T(8,128)(2,1)}), bf16[72,4608]{1,0:T(8,128)(2,1)}) %reduce-scatter.9.cloned.1.call-update) | async-done | bytes 663568
  438.8 4.6 all-to-all-start.5
  453.7 3.1 multiply_convert_fusion.6
  460.8 3.9 multiply_convert_fusion.2
  471.1 3.3 collective-permute-done.10
  478.6 2.7 convert_add_fusion.3
  481.3 2.3 copy.278
  483.6 2.9 maximum_select_fusion
  487.7 2.3 copy.280
  489.9 5.0 reshape.287
  495.0 2.9 multiply_convert_fusion.4
  499.7 3.5 convert_add_fusion
  505.0 3.2 multiply_convert_fusion.3
  508.3 2.6 convert_add_fusion.2
  510.9 5.9 %collective-permute-done.13 = bf16[288,576]{1,0:T(8,128)(2,1)S(1)} collective-permute-done((bf16[288,576]{1,0:T(8,128)(2,1)S(1)}, bf16[288,576]{1,0:T(8,128)(2,1)S(1)}, u32[]{:S(2)}, u32[]{:S(2)}) %collective-permute-start.13) | collective-permute-done | bytes 331808 | tf_op jit(solution)/shard_map/ppermute | solution.py:109
  (332 shorter events, 116.1 us)
Async XLA Ops:
  7.2 72.2 %all-gather.3.cloned.1.call-start = ((), (), s32[]{:S(2)}) async-start(), calls=%async_computation.8 | async-start | bytes 7206912 | tf_op jit(solution)/shard_map/all_gather | solution.py:139
  10.3 159.0 %all-gather.5.cloned.1.call-start = ((), (), s32[]{:S(2)}) async-start(), calls=%async_computation.9 | async-start | bytes 11280384 | tf_op jit(solution)/shard_map/all_gather | solution.py:148
  15.7 12.4 %copy-start.1 = (bf16[1,128,1152]{2,1,0:T(8,128)(2,1)S(1)}, bf16[1,128,1152]{2,1,0:T(8,128)(2,1)}, u32[]{:S(2)}) copy-start(bf16[1,128,1152]{2,1,0:T(8,128)(2,1)} %param.22) | copy-start | bytes 884740
  16.6 20.6 %copy-start = (f32[1152,432]{0,1:T(8,128)S(1)}, f32[1152,432]{0,1:T(8,128)}, u32[]{:S(2)}) copy-start(f32[1152,432]{0,1:T(8,128)} %param.30) | copy-start | bytes 5971972
  20.7 16.2 %all-to-all-start = ((bf16[32,2,576]{2,1,0:T(2,128)(2,1)}), bf16[32,2,576]{2,1,0:T(2,128)(2,1)S(1)}, u32[]{:S(2)}, u32[]{:S(2)}) async-start(bf16[32,2,576]{2,1,0:T(2,128)(2,1)} %reshape.315), calls=%async_computation | async-start | bytes 163840 | tf_op jit(solution)/shard_map/all_to_all | solution.py:122
  28.2 20.7 %copy-start.55 = (f32[128]{0:T(128)}, f32[128]{0:T(128)S(1)}, u32[]{:S(2)}) copy-start(f32[128]{0:T(128)S(1)} %broadcast_multiply_fusion.5) | copy-start | bytes 1540
  37.1 5.2 copy-start.35
  38.2 10.4 %all-to-all-start.1 = ((f32[16,1,432]{2,1,0:T(1,128)}), f32[16,1,432]{2,1,0:T(1,128)S(1)}, u32[]{:S(2)}, u32[]{:S(2)}) async-start(f32[16,1,432]{2,1,0:T(1,128)} %copy.246), calls=%async_computation.1 | async-start | bytes 65536 | tf_op jit(solution)/shard_map/all_to_all | solution.py:158
  41.9 300.0 %reduce-scatter.7.cloned.1.call-start = ((), (), s32[]{:S(2)}) async-start(), calls=%async_computation.10 | async-start | bytes 5640192
  42.2 7.0 %copy-start.57 = (f32[128]{0:T(128)}, f32[128]{0:T(128)S(1)}, u32[]{:S(2)}) copy-start(f32[128]{0:T(128)S(1)} %add_rsqrt_fusion.1) | copy-start | bytes 1540
  49.2 34.3 %copy-start.19 = (bf16[128,1152]{1,0:T(8,128)(2,1)}, bf16[128,1152]{1,0:T(8,128)(2,1)S(1)}, u32[]{:S(2)}) copy-start(bf16[128,1152]{1,0:T(8,128)(2,1)S(1)} %fusion.50) | copy-start | bytes 884740
  49.2 8.8 %collective-permute-start = (bf16[128,1152]{1,0:T(8,128)(2,1)S(1)}, bf16[128,1152]{1,0:T(8,128)(2,1)S(1)}, u32[]{:S(2)}, u32[]{:S(2)}) collective-permute-start(bf16[128,1152]{1,0:T(8,128)(2,1)S(1)} %fusion.50), channel_id=1, source_target_pairs={{0,16},{16,0},{1,17},{17,1},{2,18},{18,2},{3,19},{19,3},{4,20},{20... | collective-permute-start | bytes 884744 | tf_op jit(solution)/shard_map/ppermute | solution.py:109
  57.9 21.5 %copy-start.43 = (bf16[128,1152]{1,0:T(8,128)(2,1)}, bf16[128,1152]{1,0:T(8,128)(2,1)S(1)}, u32[]{:S(2)}) copy-start(bf16[128,1152]{1,0:T(8,128)(2,1)S(1)} %collective-permute-done) | copy-start | bytes 884740
  87.1 10.0 %copy-start.23 = (bf16[2,8,72,128]{3,2,1,0:T(8,128)(2,1)}, bf16[2,8,72,128]{3,2,1,0:T(8,128)(2,1)S(1)}, u32[]{:S(2)}) copy-start(bf16[2,8,72,128]{3,2,1,0:T(8,128)(2,1)S(1)} %convolution_convert_fusion.7) | copy-start | bytes 884740
  87.1 9.2 %collective-permute-start.1 = (bf16[2,128,576]{1,2,0:T(8,128)(2,1)S(1)}, bf16[2,128,576]{1,2,0:T(8,128)(2,1)S(1)}, u32[]{:S(2)}, u32[]{:S(2)}) collective-permute-start(bf16[2,128,576]{1,2,0:T(8,128)(2,1)S(1)} %bitcast.156), channel_id=1, source_target_pairs={{0,16},{16,0},{1,17},{17,1},{2,18},{18,2},{3,19},{19,3},{4,20},{20... | collective-permute-start | bytes 884744 | tf_op jit(solution)/shard_map/ppermute | solution.py:109
  100.8 71.4 %copy-start.10 = (bf16[128,1152]{1,0:T(8,128)(2,1)}, bf16[128,1152]{1,0:T(8,128)(2,1)S(1)}, u32[]{:S(2)}) copy-start(bf16[128,1152]{1,0:T(8,128)(2,1)S(1)} %add_convert_fusion) | copy-start | bytes 884740
  100.8 9.9 %collective-permute-start.2 = (bf16[128,1152]{1,0:T(8,128)(2,1)S(1)}, bf16[128,1152]{1,0:T(8,128)(2,1)S(1)}, u32[]{:S(2)}, u32[]{:S(2)}) collective-permute-start(bf16[128,1152]{1,0:T(8,128)(2,1)S(1)} %add_convert_fusion), channel_id=1, source_target_pairs={{0,16},{16,0},{1,17},{17,1},{2,18},{18,2},{3,19},{19,3},{4,20},{20... | collective-permute-start | bytes 884744 | tf_op jit(solution)/shard_map/ppermute | solution.py:109
  103.1 73.0 %collective-permute-start.4 = (bf16[128,1152]{1,0:T(8,128)(2,1)}, bf16[128,1152]{1,0:T(8,128)(2,1)}, u32[]{:S(2)}, u32[]{:S(2)}) collective-permute-start(bf16[128,1152]{1,0:T(8,128)(2,1)} %fusion.47), channel_id=1, source_target_pairs={{0,16},{16,0},{1,17},{17,1},{2,18},{18,2},{3,19},{19,3},{4,20},{20... | collective-permute-start | bytes 884744 | tf_op jit(solution)/shard_map/ppermute | solution.py:109
  110.8 61.5 %copy-start.31 = (bf16[128,1152]{1,0:T(8,128)(2,1)}, bf16[128,1152]{1,0:T(8,128)(2,1)S(1)}, u32[]{:S(2)}) copy-start(bf16[128,1152]{1,0:T(8,128)(2,1)S(1)} %collective-permute-done.2) | copy-start | bytes 884740
  169.3 6.8 %copy-start.34 = (bf16[1152,4608]{1,0:T(8,128)(2,1)S(1)}, bf16[1152,4608]{1,0:T(8,128)(2,1)}, u32[]{:S(2)}) copy-start(bf16[1152,4608]{1,0:T(8,128)(2,1)} %all-gather.5.cloned.1.call-done) | copy-start | bytes 31850500
  172.3 13.9 %copy-start.62 = (f32[256,1152]{1,0:T(8,128)}, f32[256,1152]{1,0:T(8,128)S(1)}, u32[]{:S(2)}) copy-start(f32[256,1152]{1,0:T(8,128)S(1)} %convolution_add_fusion.3) | copy-start | bytes 3538948
  176.2 11.1 %copy-start.64 = (f32[256,1152]{1,0:T(8,128)}, f32[256,1152]{1,0:T(8,128)S(1)}, u32[]{:S(2)}) copy-start(f32[256,1152]{1,0:T(8,128)S(1)} %convolution_add_fusion.2) | copy-start | bytes 3538948
  184.6 9.9 %collective-permute-start.5 = (bf16[128,1152]{1,0:T(8,128)(2,1)S(1)}, bf16[128,1152]{1,0:T(8,128)(2,1)S(1)}, u32[]{:S(2)}, u32[]{:S(2)}) collective-permute-start(bf16[128,1152]{1,0:T(8,128)(2,1)S(1)} %slice.300), channel_id=1, source_target_pairs={{0,16},{16,0},{1,17},{17,1},{2,18},{18,2},{3,19},{19,3},{4,20},{20... | collective-permute-start | bytes 884744 | tf_op jit(solution)/shard_map/ppermute | solution.py:109
  188.7 11.4 %copy-start.12 = (f32[128,1152]{1,0:T(8,128)S(1)}, f32[128,1152]{1,0:T(8,128)}, u32[]{:S(2)}) copy-start(f32[128,1152]{1,0:T(8,128)} %get-tuple-element.250) | copy-start | bytes 1769476
  188.8 11.4 %copy-start.18 = (bf16[1,128,1152]{2,1,0:T(8,128)(2,1)S(1)}, bf16[1,128,1152]{2,1,0:T(8,128)(2,1)}, u32[]{:S(2)}) copy-start(bf16[1,128,1152]{2,1,0:T(8,128)(2,1)} %param.25) | copy-start | bytes 884740
  188.8 11.4 %collective-permute-start.3 = (bf16[128,1152]{1,0:T(8,128)(2,1)S(1)}, bf16[128,1152]{1,0:T(8,128)(2,1)S(1)}, u32[]{:S(2)}, u32[]{:S(2)}) collective-permute-start(bf16[128,1152]{1,0:T(8,128)(2,1)S(1)} %slice.301), channel_id=1, source_target_pairs={{0,16},{16,0},{1,17},{17,1},{2,18},{18,2},{3,19},{19,3},{4,20},{20... | collective-permute-start | bytes 884744 | tf_op jit(solution)/shard_map/ppermute | solution.py:109
  202.2 8.4 %copy-start.45 = (bf16[128,1152]{1,0:T(8,128)(2,1)}, bf16[128,1152]{1,0:T(8,128)(2,1)S(1)}, u32[]{:S(2)}) copy-start(bf16[128,1152]{1,0:T(8,128)(2,1)S(1)} %multiply_convert_fusion.5) | copy-start | bytes 884740
  202.2 9.1 %slice-start = ((bf16[1152,2880]{1,0:T(8,128)(2,1)}), bf16[1152,1152]{1,0:T(8,128)(2,1)S(1)}, s32[]{:S(2)}) async-start(bf16[1152,2880]{1,0:T(8,128)(2,1)} %all-gather.3.cloned.1.call-done), calls=%async_computation.12 | async-start | bytes 5308416 | tf_op jit(solution)/shard_map/slice | solution.py:140
  202.2 8.4 %collective-permute-start.6 = (bf16[128,1152]{1,0:T(8,128)(2,1)S(1)}, bf16[128,1152]{1,0:T(8,128)(2,1)S(1)}, u32[]{:S(2)}, u32[]{:S(2)}) collective-permute-start(bf16[128,1152]{1,0:T(8,128)(2,1)S(1)} %multiply_convert_fusion.5), channel_id=1, source_target_pairs={{0,16},{16,0},{1,17},{17,1},{2,18},{18,2},{3,19},{19,3},{4,20},{20... | collective-permute-start | bytes 884744 | tf_op jit(solution)/shard_map/ppermute | solution.py:109
  204.6 9.1 %copy-start.24 = (bf16[2,8,72,128]{3,2,1,0:T(8,128)(2,1)S(1)}, bf16[2,8,72,128]{3,2,1,0:T(8,128)(2,1)}, u32[]{:S(2)}) copy-start(bf16[2,8,72,128]{3,2,1,0:T(8,128)(2,1)} %copy-done.23) | copy-start | bytes 884740
  232.7 200.0 %reduce-scatter.9.cloned.1.call-start = ((), (), s32[]{:S(2)}) async-start(), calls=%async_computation.11 | async-start | bytes 11280384
  295.7 9.2 %collective-permute-start.7 = (bf16[128,1152]{1,0:T(8,128)(2,1)S(1)}, bf16[128,1152]{1,0:T(8,128)(2,1)S(1)}, u32[]{:S(2)}, u32[]{:S(2)}) collective-permute-start(bf16[128,1152]{1,0:T(8,128)(2,1)S(1)} %slice.299), channel_id=1, source_target_pairs={{0,16},{16,0},{1,17},{17,1},{2,18},{18,2},{3,19},{19,3},{4,20},{20... | collective-permute-start | bytes 884744 | tf_op jit(solution)/shard_map/ppermute | solution.py:109
  311.0 9.8 %all-to-all-start.2 = ((bf16[32,2,216]{2,1,0:T(2,128)(2,1)}), bf16[32,2,216]{2,1,0:T(2,128)(2,1)S(1)}, u32[]{:S(2)}, u32[]{:S(2)}) async-start(bf16[32,2,216]{2,1,0:T(2,128)(2,1)} %reshape.317), calls=%async_computation.2 | async-start | bytes 65536 | tf_op jit(solution)/shard_map/all_to_all | solution.py:263
  320.8 10.0 %all-to-all-start.4 = ((f32[32,1,504]{2,1,0:T(1,128)}), f32[32,1,504]{2,1,0:T(1,128)S(1)}, u32[]{:S(2)}, u32[]{:S(2)}) async-start(f32[32,1,504]{2,1,0:T(1,128)} %all_to_all.52), calls=%async_computation.4 | async-start | bytes 131072 | tf_op jit(solution)/shard_map/all_to_all | solution.py:287
  323.6 10.8 %copy-start.36 = (bf16[32,1,1152]{2,1,0:T(2,128)(2,1)S(1)}, bf16[32,1,1152]{2,1,0:T(2,128)(2,1)}, u32[]{:S(2)}) copy-start(bf16[32,1,1152]{2,1,0:T(2,128)(2,1)} %copy-done.35) | copy-start | bytes 221188
  330.8 10.5 %all-to-all-start.3 = ((f32[16,1,1152]{2,1,0:T(1,128)}), f32[16,1,1152]{2,1,0:T(1,128)S(1)}, u32[]{:S(2)}, u32[]{:S(2)}) async-start(f32[16,1,1152]{2,1,0:T(1,128)} %copy.267), calls=%async_computation.3 | async-start | bytes 147456 | tf_op jit(solution)/shard_map/all_to_all | solution.py:269
  334.4 7.0 %copy-start.51 = (f32[1,1152]{1,0:T(1,128)S(1)}, f32[1,1152]{1,0:T(1,128)}, u32[]{:S(2)}) copy-start(f32[1,1152]{1,0:T(1,128)} %get-tuple-element.210) | copy-start | bytes 13828
  334.4 7.0 %copy-start.52 = (f32[1,1152]{1,0:T(1,128)S(1)}, f32[1,1152]{1,0:T(1,128)}, u32[]{:S(2)}) copy-start(f32[1,1152]{1,0:T(1,128)} %get-tuple-element.211) | copy-start | bytes 13828
  343.6 99.8 %collective-permute-start.8 = (bf16[72,3,576]{2,1,0:T(4,128)(2,1)S(1)}, bf16[72,3,576]{2,1,0:T(4,128)(2,1)}, u32[]{:S(2)}, u32[]{:S(2)}) collective-permute-start(bf16[72,3,576]{2,1,0:T(4,128)(2,1)S(1)} %copy.269), channel_id=1, source_target_pairs={{0,16},{16,0},{1,17},{17,1},{2,18},{18,2},{3,19},{19,3},{4,20},{20... | collective-permute-start | bytes 746504 | tf_op jit(solution)/shard_map/ppermute | solution.py:109
  438.8 11.9 %all-to-all-start.5 = ((f32[32,1,505]{2,1,0:T(1,128)}), f32[32,1,505]{2,1,0:T(1,128)}, u32[]{:S(2)}, u32[]{:S(2)}) async-start(f32[32,1,505]{2,1,0:T(1,128)} %broadcast_in_dim.121), calls=%async_computation.5 | async-start | bytes 131072 | tf_op jit(solution)/shard_map/all_to_all | solution.py:122
  447.6 33.7 %collective-permute-start.11 = (bf16[72,1,4608]{2,0,1:T(8,128)(2,1)}, bf16[72,1,4608]{2,0,1:T(8,128)(2,1)}, u32[]{:S(2)}, u32[]{:S(2)}) collective-permute-start(bf16[72,1,4608]{2,0,1:T(8,128)(2,1)} %copy.277), channel_id=1, source_target_pairs={{0,16},{16,0},{1,17},{17,1},{2,18},{18,2},{3,19},{19,3},{4,20},{20... | collective-permute-start | bytes 1990664 | tf_op jit(solution)/shard_map/ppermute | solution.py:109
  453.7 7.1 %copy-start.3 = (f32[1152,432]{0,1:T(8,128)S(1)}, f32[1152,432]{0,1:T(8,128)}, u32[]{:S(2)}) copy-start(f32[1152,432]{0,1:T(8,128)} %copy-done.2) | copy-start | bytes 5971972
  456.8 21.8 %collective-permute-start.9 = (bf16[72,1728]{1,0:T(8,128)(2,1)}, bf16[72,1728]{1,0:T(8,128)(2,1)}, u32[]{:S(2)}, u32[]{:S(2)}) collective-permute-start(bf16[72,1728]{1,0:T(8,128)(2,1)} %get-tuple-element.203), channel_id=1, source_target_pairs={{0,16},{16,0},{1,17},{17,1},{2,18},{18,2},{3,19},{19,3},{4,20},{20... | collective-permute-start | bytes 746504 | tf_op jit(solution)/shard_map/ppermute | solution.py:109
  459.4 7.5 %copy-start.42 = (f32[16128]{0:T(1024)S(1)}, f32[16128]{0:T(1024)}, u32[]{:S(2)}) copy-start(f32[16128]{0:T(1024)} %param.31) | copy-start | bytes 193540
  459.4 15.0 %collective-permute-start.10 = (bf16[72,576]{0,1:T(8,128)(2,1)}, bf16[72,576]{0,1:T(8,128)(2,1)}, u32[]{:S(2)}, u32[]{:S(2)}) collective-permute-start(bf16[72,576]{0,1:T(8,128)(2,1)} %get-tuple-element.200), channel_id=1, source_target_pairs={{0,16},{16,0},{1,17},{17,1},{2,18},{18,2},{3,19},{19,3},{4,20},{20... | collective-permute-start | bytes 248840 | tf_op jit(solution)/shard_map/ppermute | solution.py:109
  464.6 35.1 %collective-permute-start.14 = (bf16[576,432]{0,1:T(8,128)(2,1)}, bf16[576,432]{0,1:T(8,128)(2,1)}, u32[]{:S(2)}, u32[]{:S(2)}) collective-permute-start(bf16[576,432]{0,1:T(8,128)(2,1)} %get-tuple-element.191), channel_id=1, source_target_pairs={{0,16},{16,0},{1,17},{17,1},{2,18},{18,2},{3,19},{19,3},{4,20},{20... | collective-permute-start | bytes 1493000 | tf_op jit(solution)/shard_map/ppermute | solution.py:109
  497.8 10.5 %collective-permute-start.12 = (bf16[72,2304]{1,0:T(8,128)(2,1)}, bf16[72,2304]{1,0:T(8,128)(2,1)}, u32[]{:S(2)}, u32[]{:S(2)}) collective-permute-start(bf16[72,2304]{1,0:T(8,128)(2,1)} %get-tuple-element.197), channel_id=1, source_target_pairs={{0,16},{16,0},{1,17},{17,1},{2,18},{18,2},{3,19},{19,3},{4,20},{20... | collective-permute-start | bytes 995336 | tf_op jit(solution)/shard_map/ppermute | solution.py:109
  508.2 8.6 %collective-permute-start.13 = (bf16[288,576]{1,0:T(8,128)(2,1)S(1)}, bf16[288,576]{1,0:T(8,128)(2,1)S(1)}, u32[]{:S(2)}, u32[]{:S(2)}) collective-permute-start(bf16[288,576]{1,0:T(8,128)(2,1)S(1)} %get-tuple-element.194), channel_id=1, source_target_pairs={{0,16},{16,0},{1,17},{17,1},{2,18},{18,2},{3,19},{19,3},{4,20},{20... | collective-permute-start | bytes 995336 | tf_op jit(solution)/shard_map/ppermute | solution.py:109
  (46 other events, 88.8 us)
Sparse Core Ops, SparseCore 0:
  10.7 68.6 all-gather.2
  82.3 87.0 all-gather.4
  232.8 76.2 reduce-scatter.6
  313.0 119.5 reduce-scatter.8

commit v2 on v1

--- a/solution.py
+++ b/solution.py
@@ -3,6 +3,8 @@
 import jax
 import jax.numpy as jnp
 from jax import lax
+from jax.experimental import pallas as pl
+from jax.experimental.pallas import tpu as pltpu
 from jax.sharding import PartitionSpec as P
 
 HD = 72
@@ -64,6 +66,91 @@
     second_hat = second_new / (1.0 - beta_two**step_count)
     change = -learn_rate * (first_hat / (jnp.sqrt(second_hat) + adam_eps) + decay_rate * weight)
     return (change, first_new, second_new)
+
+
+def outer(left, right):
+    return lax.dot_general(
+        left, right, (((0,), (0,)), ((), ())), preferred_element_type=jnp.float32
+    ).astype(jnp.bfloat16)
+
+
+def pack_products(pairs, picks, starts, total, block):
+    lefts, rights = pairs
+    tall, width = lefts[0].shape
+    wide = total // len(picks)
+
+    def body(*refs):
+        step = pl.program_id(0)
+        out = refs[-1]
+        for j, writes in enumerate(picks):
+
+            @pl.when(step == j)
+            def _():
+                for left, right, column in writes:
+                    value = outer(refs[left][...], refs[len(lefts) + right][...])
+                    out[:, column : column + value.shape[1]] = value
+
+    return pl.pallas_call(
+        body,
+        grid=(len(picks), width // block),
+        in_specs=[pl.BlockSpec((tall, block), lambda j, i: (0, i)) for _ in lefts]
+        + [pl.BlockSpec(r.shape, lambda j, i: (0, 0)) for r in rights],
+        out_specs=pl.BlockSpec((block, wide), lambda j, i: (i, j)),
+        out_shape=jax.ShapeDtypeStruct((width, total), jnp.bfloat16),
+        name=starts,
+    )(*lefts, *rights)
+
+
+def update_both(weight, grads, first, second, first_far, second_far, scalars, plan):
+    size, blocks = plan
+    clip, turn = scalars
+
+    def cut(ref, start):
+        return ref[:, start : start + size]
+
+    def put(ref, start, value):
+        ref[:, start : start + size] = value
+
+    def body(clip_ref, turn_ref, w_ref, *refs):
+        g_refs = refs[: len(grads)]
+        m_ref, v_ref, mf_ref, vf_ref, w_out, m_out, v_out = refs[len(grads) :]
+        scale = clip_ref[0]
+        for place in (0, 1):
+
+            @pl.when(turn_ref[0] == place)
+            def _():
+                for w_at, g_member, g_at, m_member, m_at in blocks:
+                    source = g_refs[0] if g_member in (-1, place) else g_refs[1]
+                    grad = cut(source, g_at).astype(jnp.float32) * scale
+                    own = m_member == place
+                    first_old = cut(m_ref if own else mf_ref, m_at)
+                    second_old = cut(v_ref if own else vf_ref, m_at)
+                    if own:
+                        put(m_out, m_at, beta_one * first_old + (1.0 - beta_one) * grad)
+                        put(v_out, m_at, beta_two * second_old + (1.0 - beta_two) * grad * grad)
+                        first_old = first_old.astype(jnp.bfloat16)
+                        second_old = second_old.astype(jnp.bfloat16)
+                    first_new = beta_one * first_old.astype(jnp.float32) + (1.0 - beta_one) * grad
+                    second_new = (
+                        beta_two * second_old.astype(jnp.float32) + (1.0 - beta_two) * grad * grad
+                    )
+                    first_hat = first_new / (1.0 - beta_one**step_count)
+                    second_hat = second_new / (1.0 - beta_two**step_count)
+                    old = cut(w_ref, w_at)
+                    change = -learn_rate * (
+                        first_hat / (jnp.sqrt(second_hat) + adam_eps) + decay_rate * old
+                    )
+                    put(w_out, w_at, old + change)
+
+    vmem = pl.BlockSpec(memory_space=pltpu.VMEM)
+    smem = pl.BlockSpec(memory_space=pltpu.SMEM)
+    return pl.pallas_call(
+        body,
+        in_specs=[smem, smem] + [vmem] * (5 + len(grads)),
+        out_specs=[vmem] * 3,
+        out_shape=[jax.ShapeDtypeStruct(a.shape, a.dtype) for a in (weight, first, second)],
+        name="update",
+    )(clip, turn, weight, *grads, first, second, first_far, second_far)
 
 
 def shards(
@@ -190,8 +277,6 @@
     a_two = (n_two * (1.0 + scale2) + shift2).astype(jnp.bfloat16)
     a_two2 = jnp.concatenate([a_two, swap(a_two)], axis=0)
 
-    mlp_sum = 0.0
-    d_a2_sum = 0.0
     g_one = []
     g_two = []
     g_b_one = []
@@ -199,17 +284,24 @@
         pre = product("ld,df->lf", a_two2, w1_b[f]) + b_one[f]
         act_val, act_slope = gelu_parts(pre)
         act = act_val.astype(jnp.bfloat16)
-        mlp_sum = mlp_sum + product("lf,fd->ld", act, w2_b[f])
         d_pre = product("ld,fd->lf", d_mlp2, w2_b[f]) * act_slope
         d_pre_b = d_pre.astype(jnp.bfloat16)
-        d_a2_sum = d_a2_sum + product("lf,df->ld", d_pre_b, w1_b[f])
-        g_one.append(product("ld,lf->df", a_two2, d_pre_b).astype(jnp.bfloat16))
-        g_two.append(product("lf,ld->fd", act, d_mlp2).astype(jnp.bfloat16))
+        g_one.append(d_pre_b)
+        g_two.append(act)
         g_b_one.append(jnp.sum(d_pre, axis=0))
-    grads_mlp = lax.psum_scatter(
-        jnp.concatenate(g_one + g_two, axis=1), "shard", scatter_dimension=0, tiled=True
-    )
-    d_a2 = d_a2_sum[:length] + swap(d_a2_sum[length:].astype(jnp.bfloat16)).astype(jnp.float32)
+    picks = [[(0, f, 0)] for f in range(folds)] + [[(1 + f, folds, 0)] for f in range(folds)]
+    pack_mlp_grad = pack_products(
+        ([a_two2] + g_two, g_one + [d_mlp2]), picks, "pack_mlp", 2 * folds * width, width
+    )
+    g_one, g_two, pack_mlp_grad = lax.optimization_barrier((g_one, g_two, pack_mlp_grad))
+    mlp_sum = 0.0
+    d_a2_sum = 0.0
+    for f in range(folds):
+        d_a2_sum = d_a2_sum + product("lf,df->ld", g_one[f], w1_b[f])
+        mlp_sum = mlp_sum + product("lf,fd->ld", g_two[f], w2_b[f])
+    d_a2_far = swap(d_a2_sum[length:].astype(jnp.bfloat16))
+    grads_mlp = lax.psum_scatter(pack_mlp_grad, "shard", scatter_dimension=0, tiled=True)
+    d_a2 = d_a2_sum[:length] + d_a2_far.astype(jnp.float32)
     mlp = (
         mlp_sum[:length]
         + swap(mlp_sum[length:].astype(jnp.bfloat16)).astype(jnp.float32)
@@ -233,7 +325,6 @@
     heads_all = jnp.concatenate(
         [heads_own, ordered(heads_flat[1], heads_other[1], 1)], axis=0
     )
-    g_proj = product("le,ld->ed", heads_all, own_half(d_attn2, 1)).astype(jnp.bfloat16)
     delta = jnp.sum(d_heads.astype(jnp.float32) * heads_out.astype(jnp.float32), axis=-1)
     delta = jnp.transpose(delta, (0, 2, 1))[..., None]
     d_probs = product("bqhd,bkhd->bhqk", d_heads, value_rows)
@@ -247,10 +338,22 @@
         [piece.astype(jnp.bfloat16).reshape(2 * length, half) for piece in (d_q, d_k, d_v)],
         axis=1,
     )
-    g_qkv = product("ld,le->de", a_one2, d_qkv).astype(jnp.bfloat16)
-    grads_attn = lax.psum_scatter(
-        jnp.concatenate([g_proj, g_qkv], axis=1), "shard", scatter_dimension=0, tiled=True
-    )
+    proj_wide = -(-half // 128) * 128
+    d_attn_half = jnp.pad(own_half(d_attn2, 1), ((0, 0), (0, proj_wide - half)))
+    pack_attn_grad = pack_products(
+        ([heads_all, a_one2], [d_attn_half, d_qkv]),
+        [[(0, 0, 0), (1, 1, proj_wide)]],
+        "pack_attn",
+        proj_wide + 3 * half,
+        3 * 128,
+    )
+    firsts = (m_qkv, m_proj, m_fc1, m_fc2, m_ada.T)
+    seconds = (v_qkv, v_proj, v_fc1, v_fc2, v_ada.T)
+    fars = []
+    if replicas == 2:
+        fars = [swap(value.astype(jnp.bfloat16)) for value in firsts + seconds]
+    fars, grads_mlp, pack_attn_grad = lax.optimization_barrier((fars, grads_mlp, pack_attn_grad))
+    grads_attn = lax.psum_scatter(pack_attn_grad, "shard", scatter_dimension=0, tiled=True)
     d_a1_sum = product("le,de->ld", d_qkv, wq_b)
     d_a1 = d_a1_sum[:length] + swap(d_a1_sum[length:].astype(jnp.bfloat16)).astype(jnp.float32)
     d_shift1 = jnp.sum(d_a1, axis=0)
@@ -263,7 +366,7 @@
     d_mod_cols = lax.all_to_all(
         d_mod_b.reshape(devices, d_mod_b.shape[2]), axes, split_axis=0, concat_axis=0, tiled=True
     )
-    g_ada = jnp.dot(silu_all.T, d_mod_cols, preferred_element_type=jnp.float32)
+    g_ada = jnp.dot(d_mod_cols.T, silu_all, preferred_element_type=jnp.float32)
     group_cols = lax.dynamic_slice_in_dim(d_mod_cols, rank * parts, parts, 0)
     silu_terms = jnp.dot(group_cols, ada_local.T, preferred_element_type=jnp.float32)
     silu_terms = lax.all_to_all(silu_terms, "shard", split_axis=0, concat_axis=0, tiled=True)
@@ -289,65 +392,79 @@
     )
     bias_chunk = jnp.sum(bias_terms, axis=0)
 
-    def complete(own):
-        return swap(own) if replicas == 2 else jnp.zeros_like(own)
-
-    def share(own, axis):
-        if replicas == 2:
-            return own
-        return lax.psum_scatter(
-            own.astype(jnp.float32), "rep", scatter_dimension=axis, tiled=True
+    count_ada = width // replicas
+    own_ada = lax.dynamic_slice_in_dim(g_ada, rank * count_ada, count_ada, 1)
+    far_mlp = swap(grads_mlp) if replicas == 2 else jnp.zeros_like(grads_mlp)
+    both_mlp = jnp.where(turn == 0, jnp.stack([grads_mlp, far_mlp]), jnp.stack([far_mlp, grads_mlp]))
+    full_one = both_mlp[:, :, : folds * width].reshape(2, rows, folds, parts, unit)
+    full_one = jnp.transpose(full_one, (1, 3, 0, 2, 4)).reshape(rows, FF)
+    full_two = both_mlp[:, :, folds * width :].reshape(2, rows, folds, width)
+    full_two = jnp.transpose(full_two, (0, 2, 1, 3)).reshape(2 * folds * rows, width)
+
+    weights = (w_qkv, w_proj, w_fc1, w_fc2, w_ada.T)
+    if replicas == 2:
+        early = sum((jnp.sum(jnp.square(g.astype(jnp.float32))) for g in (grads_mlp, own_ada)))
+        early = early + jnp.sum(bias_chunk * bias_chunk)
+        grads_attn, full_one, full_two, g_ada, early = lax.optimization_barrier(
+            (grads_attn, full_one, full_two, g_ada, early)
         )
-
-    def split(value):
-        if replicas == 2:
-            return own_half(value, 1)
-        return share(value, 1)
-
-    own_proj = grads_attn[:, :half]
-    if replicas > 2:
-        own_proj = share(ordered(own_proj, jnp.zeros_like(own_proj), 1), 1)
-    own_qkv = grads_attn[:, half:].reshape(rows, 3, half)
-    full_qkv = ordered(own_qkv, complete(own_qkv), 2).reshape(rows, 3 * inner)
-    own_mlp = grads_mlp[:, None]
-    full_mlp_grad = ordered(own_mlp, complete(own_mlp), 1)
-    full_one = full_mlp_grad[:, :, : folds * width].reshape(rows, 2, folds, parts, unit)
-    full_one = jnp.transpose(full_one, (0, 3, 1, 2, 4)).reshape(rows, FF)
-    full_two = full_mlp_grad[:, :, folds * width :].reshape(rows, 2, folds, width)
-    full_two = jnp.transpose(full_two, (1, 2, 0, 3)).reshape(2 * folds * rows, width)
-    count_ada = width // replicas
-    own_ada = lax.dynamic_slice_in_dim(g_ada, rank * count_ada, count_ada, 0)
-    pieces = [split(full_qkv), own_proj, split(full_one), split(full_two), own_ada]
-    pieces = [piece.astype(jnp.float32) for piece in pieces]
-    if replicas == 2:
-        counted = [grads_attn.astype(jnp.float32), grads_mlp.astype(jnp.float32), own_ada]
+        counted = [grads_attn.astype(jnp.float32)]
     else:
+        blank = jnp.zeros_like(grads_attn)
+        both = ordered(grads_attn[None], blank[None], 0)
+        full_proj = jnp.transpose(both[:, :, :half], (1, 0, 2)).reshape(rows, inner)
+        full_qkv = both[:, :, proj_wide:].reshape(2, rows, 3, half)
+        full_qkv = jnp.transpose(full_qkv, (1, 2, 0, 3)).reshape(rows, 3 * inner)
+        pieces = [
+            lax.psum_scatter(full.astype(jnp.float32), "rep", scatter_dimension=1, tiled=True)
+            for full in (full_qkv, full_proj, full_one, full_two)
+        ] + [own_ada]
         counted = pieces
-    squares = sum((jnp.sum(p * p) for p in counted)) + jnp.sum(bias_chunk * bias_chunk)
+        early = jnp.sum(bias_chunk * bias_chunk)
+    squares = sum((jnp.sum(p * p) for p in counted)) + early
     totals = spread(jnp.concatenate([bias_chunk, squares[None]])[None])
     g_bias = totals[:, :chunk].reshape(devices * chunk)
     gnorm = jnp.sqrt(jnp.sum(totals[:, chunk]))
     clip = 1.0 / jnp.maximum(gnorm, 1.0)
 
-    weights = (w_qkv, w_proj, w_fc1, w_fc2, w_ada)
-    dims = (1, 1, 1, 1, 0)
-    firsts = (m_qkv, m_proj, m_fc1, m_fc2, m_ada)
-    seconds = (v_qkv, v_proj, v_fc1, v_fc2, v_ada)
     new_w = []
     new_m = []
     new_v = []
-    for weight, dim, grad, first, second in zip(weights, dims, pieces, firsts, seconds):
-        count = weight.shape[dim] // replicas
-        own = lax.dynamic_slice_in_dim(weight, rank * count, count, dim)
-        change, first_new, second_new = adam_change(own, grad, first, second, clip)
-        change = change.astype(jnp.bfloat16)
-        if replicas == 2:
-            changes = ordered(change, swap(change), dim)
-        else:
-            changes = lax.all_gather(change, "rep", axis=dim, tiled=True)
-        new_w.append(weight + changes.astype(jnp.float32))
-        new_m.append(first_new)
-        new_v.append(second_new)
+    if replicas == 2:
+        far_attn = swap(grads_attn)
+        scalars = (clip.reshape(1), turn.reshape(1).astype(jnp.int32))
+        pair_attn = (grads_attn, far_attn)
+        sources = (pair_attn, pair_attn, (full_one,), (full_two,), (g_ada,))
+        plans = (
+            (
+                half,
+                [
+                    (half * b, b % 2, proj_wide + half * (b // 2), b // 3, half * (b % 3))
+                    for b in range(6)
+                ],
+            ),
+            (half, [(half * b, b, 0, b, 0) for b in range(2)]),
+            (FF // 2, [(FF // 2 * b, -1, FF // 2 * b, b, 0) for b in range(2)]),
+            (half, [(half * b, -1, half * b, b, 0) for b in range(2)]),
+            (count_ada, [(count_ada * b, -1, count_ada * b, b, 0) for b in range(2)]),
+        )
+        for k, (weight, grads, plan) in enumerate(zip(weights, sources, plans)):
+            updated, first_new, second_new = update_both(
+                weight, grads, firsts[k], seconds[k], fars[k], fars[5 + k], scalars, plan
+            )
+            new_w.append(updated)
+            new_m.append(first_new)
+            new_v.append(second_new)
+    else:
+        for weight, grad, first, second in zip(weights, pieces, firsts, seconds):
+            count = weight.shape[1] // replicas
+            own = lax.dynamic_slice_in_dim(weight, rank * count, count, 1)
+            change, first_new, second_new = adam_change(own, grad, first, second, clip)
+            changes = lax.all_gather(change.astype(jnp.bfloat16), "rep", axis=1, tiled=True)
+            new_w.append(weight + changes.astype(jnp.float32))
+            new_m.append(first_new)
+            new_v.append(second_new)
+    new_w[4], new_m[4], new_v[4] = new_w[4].T, new_m[4].T, new_v[4].T
     bias_update, new_m_bias, new_v_bias = adam_change(biases, g_bias, m_bias, v_bias, clip)
     return (
         block_out,

time: 533 us -> 455 us (0.85)
  waiting for transfers between devices: 244 us -> 185 us
  Pallas kernels: 0 us -> 41 us
  other arithmetic: 88.4 us -> 48.7 us
  local copies, waits for them, and re-layouts: 84.7 us -> 53.1 us
  starting transfers between devices: 41.5 us -> 49.8 us
    unnamed x6 -> x4, waiting for transfers between devices: 87.4 us -> 0.07 us
    pallas_call x0 -> x7, Pallas kernels: none -> 41 us  [the longest x5 27.1 us: update_both(): pl.pallas_call(body, in_specs=[smem, smem] + [vmem] * (5 + len(grads)), o...]
    unnamed x164 -> x177, local copies, waits for them, and re-layouts: 54.4 us -> 14.6 us
    concatenate x2 -> x5, other arithmetic: 30.9 us -> 5.75 us  [the longest x1 1.92 us: shards(): d_mlp2 = jnp.concatenate([d_mlp_b, swap(d_mlp_b)], axis=0)]
    reduce_scatter x0 -> x1, waiting for transfers between devices: none -> 14.9 us  [shards(): lax.psum_scatter(pack_mlp_grad, 'shard', scatter_dimension=0, tiled=True)]
    add x5 -> x0, other arithmetic: 12.5 us -> none  [shards(): new_w.append(weight + changes.astype(jnp.float32))]
    optimization_barrier x0 -> x1, waiting for transfers between devices: none -> 10.4 us  [shards(): lax.optimization_barrier((grads_attn, full_one, full_two, g_ada, early))]
    reshape x2 -> x11, local copies, waits for them, and re-layouts: 5.34 us -> 15.3 us  [the longest x6 7.06 us: shards(): piece.astype(jnp.bfloat16).reshape(2 * length, half)]
  transfers between devices with their start and end apart: 25 -> 30, of which waited for: 17 -> 20; matrix products, arithmetic and copies ran while one was open for 34% -> 28% of each run, Pallas kernels for 0% -> 6%
where the time goes in v2:
time: 455 us; the launch traced here: 448 us
  waiting for transfers between devices  185 us (41%)
  local copies, waits for them, and re-layouts  53.1 us (12%)
  matrix products  50.7 us (11%)
  starting transfers between devices  49.8 us (11%)
  other arithmetic  48.7 us (11%)
  Pallas kernels  41 us (9%)
  between operations  19.6 us (4%)
    all_gather x1, waiting for transfers between devices, shards(): full_mlp = lax.all_gather(pack_mlp, 'shard', axis=0, tiled=True)  57.4 us
    ppermute x20, waiting for transfers between devices, swap(): return lax.ppermute(value, 'rep', couples)  49.1 us
    dot_general x17, matrix products, product(): return jnp.einsum(form, left, right, preferred_element_type=jnp.float32)  47.3 us
    pallas_call x5, Pallas kernels, update_both(): pl.pallas_call(body, in_specs=[smem, smem] + [vmem] * (5 + len(grads)), o...  27.1 us
    ppermute x20, starting transfers between devices, swap(): return lax.ppermute(value, 'rep', couples)  24.4 us
    all_gather x1, waiting for transfers between devices, shards(): full_attn = lax.all_gather(pack_attn, 'shard', axis=0, tiled=True)  21.3 us
    reduce_scatter x1, waiting for transfers between devices, shards(): lax.psum_scatter(pack_mlp_grad, 'shard', scatter_dimension=0, tiled=True)  14.9 us
    unnamed x177, local copies, waits for them, and re-layouts  14.6 us
  transfers between devices with their start and end apart: 30, of which 20 were waited for; matrix products, arithmetic and copies ran while one was open for 28% of the time, Pallas kernels for 6%

profile of v2, /device:TPU:0, one launch (start us, length us, event | category | flops | bytes accessed | tf_op | source)
XLA Modules:
  0.0 447.9 jit_solution(17856421860596765754)
XLA Ops:
  10.5 2.6 reshape.276
  20.6 7.3 %all-to-all-start = ((bf16[32,2,576]{2,1,0:T(2,128)(2,1)}), bf16[32,2,576]{2,1,0:T(2,128)(2,1)S(1)}, u32[]{:S(2)}, u32[]{:S(2)}) async-start(bf16[32,2,576]{2,1,0:T(2,128)(2,1)} %reshape.314), calls=%async_computation | async-start | bytes 163840 | tf_op jit(solution)/shard_map/all_to_all | solution.py:209
  28.3 8.4 %all-to-all-done = bf16[32,2,576]{2,1,0:T(2,128)(2,1)S(1)} async-done(((bf16[32,2,576]{2,1,0:T(2,128)(2,1)}), bf16[32,2,576]{2,1,0:T(2,128)(2,1)S(1)}, u32[]{:S(2)}, u32[]{:S(2)}) %all-to-all-start) | async-done | bytes 73760 | tf_op jit(solution)/shard_map/all_to_all | solution.py:209
  38.0 3.6 all-to-all-start.1
  42.1 6.2 %all-to-all-done.1 = f32[16,1,432]{2,1,0:T(1,128)S(1)} async-done(((f32[16,1,432]{2,1,0:T(1,128)}), f32[16,1,432]{2,1,0:T(1,128)S(1)}, u32[]{:S(2)}, u32[]{:S(2)}) %all-to-all-start.1) | async-done | bytes 27680 | tf_op jit(solution)/shard_map/all_to_all | solution.py:245
  51.8 6.3 %collective-permute-done = bf16[128,1152]{1,0:T(8,128)(2,1)S(1)} collective-permute-done((bf16[128,1152]{1,0:T(8,128)(2,1)S(1)}, bf16[128,1152]{1,0:T(8,128)(2,1)S(1)}, u32[]{:S(2)}, u32[]{:S(2)}) %collective-permute-start) | collective-permute-done | bytes 294944 | tf_op jit(solution)/shard_map/ppermute | solution.py:196
  58.1 21.3 %all-gather.3.cloned.1.call-done = bf16[1152,2880]{1,0:T(8,128)(2,1)} async-done(((bf16[72,2880]{1,0:T(8,128)(2,1)}), bf16[1152,2880]{1,0:T(8,128)(2,1)}) %all-gather.3.cloned.1.call-update) | async-done | bytes 6635536 | tf_op jit(solution)/shard_map/all_gather | solution.py:226
  79.4 4.0 fusion.3
  92.4 6.2 %collective-permute-done.1 = bf16[2,128,576]{2,1,0:T(8,128)(2,1)S(1)} collective-permute-done((bf16[2,128,576]{2,1,0:T(8,128)(2,1)S(1)}, bf16[2,128,576]{2,1,0:T(8,128)(2,1)S(1)}, u32[]{:S(2)}, u32[]{:S(2)}) %collective-permute-start.1) | collective-permute-done | bytes 294944 | tf_op jit(solution)/shard_map/ppermute | solution.py:196
  99.6 3.3 fusion.99
  107.0 4.1 collective-permute-done.3
  112.0 57.4 %all-gather.5.cloned.1.call-done = bf16[1152,4608]{1,0:T(8,128)(2,1)} async-done(((bf16[72,4608]{1,0:T(8,128)(2,1)}), bf16[1152,4608]{1,0:T(8,128)(2,1)}) %all-gather.5.cloned.1.call-update) | async-done | bytes 10616848 | tf_op jit(solution)/shard_map/all_gather | solution.py:235
  169.3 3.8 multiply_convert_fusion.1
  173.1 4.7 %fusion.102 = (f32[1152]{0:T(1024)}, bf16[256,1152]{1,0:T(8,128)(2,1)}) fusion(f32[256,1152]{1,0:T(8,128)S(1)} %get-tuple-element.170, bf16[1152,4608]{1,0:T(8,128)(2,1)} %all-gather.5.cloned.1.call-done, bf16[128,1152]{1,0:T(8,128)(2,1)} %collective-permute-done.2, bf16[128,1152]{1,0:T(8,128)(2,1)} %fusion.45), kind=kOutput, calls=%fused_computation.212 | convolution fusion | flops 686553984 | bytes 5018112 | tf_op jit(solution)/shard_map/ld,fd->lf/dot_general | solution.py:26
  179.6 3.6 fusion.103
  183.3 8.2 %pack_mlp.1 = bf16[1152,4608]{1,0:T(8,128)(2,1)} custom-call(bf16[256,1152]{1,0:T(8,128)(2,1)} %pad_maximum_fusion.5.refs_0_, bf16[256,1152]{1,0:T(8,128)(2,1)} %get-tuple-element.58.refs_1_, bf16[256,1152]{1,0:T(8,128)(2,1)} %get-tuple-element.59.refs_2_, bf16[256,1152]{1,0:T(8,128)(2,1)} %get-tuple-element.60.refs_3_, ...), custom_call_target="tpu_custom_call" | custom-call | tf_op jit(solution)/shard_map/pack_mlp/pallas_call | solution.py:93
  209.1 3.1 fusion.9
  212.3 3.0 convolution_add_fusion
  216.9 2.8 fusion.12
  219.7 2.8 convolution_add_fusion.1
  222.6 6.5 %collective-permute-done.5 = bf16[128,1152]{1,0:T(8,128)(2,1)S(1)} collective-permute-done((bf16[128,1152]{1,0:T(8,128)(2,1)S(1)}, bf16[128,1152]{1,0:T(8,128)(2,1)S(1)}, u32[]{:S(2)}, u32[]{:S(2)}) %collective-permute-start.5) | collective-permute-done | bytes 294944 | tf_op jit(solution)/shard_map/ppermute | solution.py:196
  231.4 6.1 %collective-permute-done.4 = bf16[128,1152]{1,0:T(8,128)(2,1)S(1)} collective-permute-done((bf16[128,1152]{1,0:T(8,128)(2,1)S(1)}, bf16[128,1152]{1,0:T(8,128)(2,1)S(1)}, u32[]{:S(2)}, u32[]{:S(2)}) %collective-permute-start.4) | collective-permute-done | bytes 294944 | tf_op jit(solution)/shard_map/ppermute | solution.py:196
  242.2 5.2 %collective-permute-done.6 = bf16[128,1152]{1,0:T(8,128)(2,1)S(1)} collective-permute-done((bf16[128,1152]{1,0:T(8,128)(2,1)S(1)}, bf16[128,1152]{1,0:T(8,128)(2,1)S(1)}, u32[]{:S(2)}, u32[]{:S(2)}) %collective-permute-start.6) | collective-permute-done | bytes 294944 | tf_op jit(solution)/shard_map/ppermute | solution.py:196
  266.2 3.1 fusion.104
  273.7 2.2 concatenate.60.refs_3_
  275.9 5.7 %pack_attn.1 = bf16[1152,2368]{1,0:T(8,128)(2,1)} custom-call(bf16[256,1152]{1,0:T(8,128)(2,1)} %pad_maximum_fusion.6.refs_0_, bf16[256,1152]{1,0:T(8,128)(2,1)} %pad_maximum_fusion.3.refs_1_, bf16[256,640]{1,0:T(8,128)(2,1)} %pad.4.refs_2_, bf16[256,1728]{1,0:T(8,128)(2,1)} %concatenate.60.refs_3_), custom_call_target="tpu_custom_call" | custom-call | tf_op jit(solution)/shard_map/pack_attn/pallas_call | solution.py:93
  281.6 2.3 collective-permute-done.11.refs_3_
  283.9 7.1 %collective-permute-done.15.refs_4_ = bf16[72,2304]{1,0:T(8,128)(2,1)} collective-permute-done((bf16[72,2304]{1,0:T(8,128)(2,1)}, bf16[72,2304]{1,0:T(8,128)(2,1)}, u32[]{:S(2)}, u32[]{:S(2)}) %collective-permute-start.15) | collective-permute-done | bytes 331808 | tf_op jit(solution)/shard_map/ppermute | solution.py:196
  291.0 4.6 %collective-permute-done.16.refs_4_ = bf16[288,576]{1,0:T(8,128)(2,1)} collective-permute-done((bf16[288,576]{1,0:T(8,128)(2,1)}, bf16[288,576]{1,0:T(8,128)(2,1)}, u32[]{:S(2)}, u32[]{:S(2)}) %collective-permute-start.16) | collective-permute-done | bytes 331808 | tf_op jit(solution)/shard_map/ppermute | solution.py:196
  295.6 14.9 %reduce-scatter.5.cloned.1.call-done = bf16[72,4608]{1,0:T(8,128)(2,1)} async-done(((bf16[1152,4608]{1,0:T(8,128)(2,1)}), bf16[72,4608]{1,0:T(8,128)(2,1)}) %reduce-scatter.5.cloned.1.call-update) | async-done | bytes 663568 | tf_op jit(solution)/shard_map/reduce_scatter | solution.py:303
  311.1 3.9 fusion.1
  339.8 3.5 all-to-all-start.2
  343.3 2.3 fusion.52
  347.3 3.7 all-to-all-done.2
  351.0 3.3 all-to-all-start.4
  358.4 3.6 all-to-all-done.4
  362.0 3.5 all-to-all-start.3
  369.6 4.6 %all-to-all-done.3 = f32[16,1,1152]{2,1,0:T(1,128)S(1)} async-done(((f32[16,1,1152]{2,1,0:T(1,128)}), f32[16,1,1152]{2,1,0:T(1,128)S(1)}, u32[]{:S(2)}, u32[]{:S(2)}) %all-to-all-start.3) | async-done | bytes 73760 | tf_op jit(solution)/shard_map/all_to_all | solution.py:372
  378.3 2.6 reshape.283
  382.3 3.2 reshape.284.refs_0_
  386.3 10.4 %reduce-scatter.7.cloned.1.call-done.refs_0_ = bf16[72,2368]{1,0:T(8,128)(2,1)} async-done(((bf16[1152,2368]{1,0:T(8,128)(2,1)}), bf16[72,2368]{1,0:T(8,128)(2,1)}) %reduce-scatter.7.cloned.1.call-update) | async-done | bytes 341008 | tf_op jit(solution)/shard_map/optimization_barrier | solution.py:408
  399.9 3.4 all-to-all-start.5
  405.7 5.1 %all-to-all-done.5 = f32[32,1,505]{2,1,0:T(1,128)S(1)} async-done(((f32[32,1,505]{2,1,0:T(1,128)}), f32[32,1,505]{2,1,0:T(1,128)S(1)}, u32[]{:S(2)}, u32[]{:S(2)}) %all-to-all-start.5) | async-done | bytes 64672 | tf_op jit(solution)/shard_map/all_to_all | solution.py:209
  412.4 5.0 %update.7 = (f32[72,4608]{1,0:T(8,128)}, f32[72,2304]{1,0:T(8,128)}, f32[72,2304]{1,0:T(8,128)}) custom-call(f32[1]{0:T(128)} %bitcast.35.clip_ref, s32[1]{0:T(128)} %bitcast.36.turn_ref, f32[72,4608]{1,0:T(8,128)} %w_ref.6, bf16[72,4608]{1,0:T(8,128)(2,1)} %reshape.284.refs_0_, f32[72,2304]{1,0:T(8,128)} %refs_1_.2, f32[72,2304]{1,0:T(8,128)} %refs_2_.6, ...), custom_call_target="tpu_custom_call" | custom-call | tf_op jit(solution)/shard_map/update/pallas_call | solution.py:147
  417.4 6.2 %update.8 = (f32[288,1152]{1,0:T(8,128)}, f32[288,576]{1,0:T(8,128)}, f32[288,576]{1,0:T(8,128)}) custom-call(f32[1]{0:T(128)} %bitcast.35.clip_ref, s32[1]{0:T(128)} %bitcast.36.turn_ref, f32[288,1152]{1,0:T(8,128)} %w_ref.7, bf16[288,1152]{1,0:T(8,128)(2,1)} %bitcast.149, f32[288,576]{1,0:T(8,128)} %refs_1_.3, f32[288,576]{1,0:T(8,128)} %refs_2_.7, ...), custom_call_target="tpu_custom_call" | custom-call | tf_op jit(solution)/shard_map/update/pallas_call | solution.py:147
  423.5 8.5 %update.9 = (f32[432,1152]{1,0:T(8,128)}, f32[432,576]{1,0:T(8,128)}, f32[432,576]{1,0:T(8,128)}) custom-call(f32[1]{0:T(128)} %bitcast.35.clip_ref, s32[1]{0:T(128)} %bitcast.36.turn_ref, f32[432,1152]{1,0:T(8,128)} %bitcast.145, f32[432,1152]{1,0:T(8,128)} %copy-done.1, f32[432,576]{1,0:T(8,128)} %bitcast.147, f32[432,576]{1,0:T(8,128)} %bitcast.148, ...), custom_call_target="tpu_custom_call" | custom-call | tf_op jit(solution)/shard_map/update/pallas_call | solution.py:147
  433.5 4.8 %update.5 = (f32[72,3456]{1,0:T(8,128)}, f32[72,1728]{1,0:T(8,128)}, f32[72,1728]{1,0:T(8,128)}) custom-call(f32[1]{0:T(128)} %bitcast.35.clip_ref, s32[1]{0:T(128)} %bitcast.36.turn_ref, f32[72,3456]{1,0:T(8,128)} %w_ref.4, bf16[72,2368]{1,0:T(8,128)(2,1)} %reduce-scatter.7.cloned.1.call-done.refs_0_, bf16[72,2368]{1,0:T(8,128)(2,1)} %copy-done.18, ...), custom_call_target="tpu_custom_call" | custom-call | tf_op jit(solution)/shard_map/update/pallas_call | solution.py:147
  438.2 2.7 update.6
  (363 shorter events, 127.6 us)
Async XLA Ops:
  7.2 72.2 %all-gather.3.cloned.1.call-start = ((), (), s32[]{:S(2)}) async-start(), calls=%async_computation.8 | async-start | bytes 7206912 | tf_op jit(solution)/shard_map/all_gather | solution.py:226
  10.3 159.0 %all-gather.5.cloned.1.call-start = ((), (), s32[]{:S(2)}) async-start(), calls=%async_computation.9 | async-start | bytes 11280384 | tf_op jit(solution)/shard_map/all_gather | solution.py:235
  16.6 20.4 %copy-start = (f32[1152,432]{0,1:T(8,128)S(1)}, f32[1152,432]{0,1:T(8,128)}, u32[]{:S(2)}) copy-start(f32[1152,432]{0,1:T(8,128)} %param.30) | copy-start | bytes 5971972
  20.6 16.1 %all-to-all-start = ((bf16[32,2,576]{2,1,0:T(2,128)(2,1)}), bf16[32,2,576]{2,1,0:T(2,128)(2,1)S(1)}, u32[]{:S(2)}, u32[]{:S(2)}) async-start(bf16[32,2,576]{2,1,0:T(2,128)(2,1)} %reshape.314), calls=%async_computation | async-start | bytes 163840 | tf_op jit(solution)/shard_map/all_to_all | solution.py:209
  28.1 21.1 %copy-start.71 = (f32[128]{0:T(128)}, f32[128]{0:T(128)S(1)}, u32[]{:S(2)}) copy-start(f32[128]{0:T(128)S(1)} %broadcast_multiply_fusion.5) | copy-start | bytes 1540
  38.0 10.2 %all-to-all-start.1 = ((f32[16,1,432]{2,1,0:T(1,128)}), f32[16,1,432]{2,1,0:T(1,128)S(1)}, u32[]{:S(2)}, u32[]{:S(2)}) async-start(f32[16,1,432]{2,1,0:T(1,128)} %copy.222), calls=%async_computation.1 | async-start | bytes 65536 | tf_op jit(solution)/shard_map/all_to_all | solution.py:245
  41.6 268.9 %reduce-scatter.5.cloned.1.call-start = ((), (), s32[]{:S(2)}) async-start(), calls=%async_computation.10 | async-start | bytes 11280384 | tf_op jit(solution)/shard_map/reduce_scatter | solution.py:303
  49.4 34.0 %copy-start.30 = (bf16[128,1152]{1,0:T(8,128)(2,1)}, bf16[128,1152]{1,0:T(8,128)(2,1)S(1)}, u32[]{:S(2)}) copy-start(bf16[128,1152]{1,0:T(8,128)(2,1)S(1)} %fusion.47) | copy-start | bytes 884740
  49.4 8.7 %collective-permute-start = (bf16[128,1152]{1,0:T(8,128)(2,1)S(1)}, bf16[128,1152]{1,0:T(8,128)(2,1)S(1)}, u32[]{:S(2)}, u32[]{:S(2)}) collective-permute-start(bf16[128,1152]{1,0:T(8,128)(2,1)S(1)} %fusion.47), channel_id=1, source_target_pairs={{0,16},{16,0},{1,17},{17,1},{2,18},{18,2},{3,19},{19,3},{4,20},{20... | collective-permute-start | bytes 884744 | tf_op jit(solution)/shard_map/ppermute | solution.py:196
  58.1 21.3 %copy-start.48 = (bf16[128,1152]{1,0:T(8,128)(2,1)}, bf16[128,1152]{1,0:T(8,128)(2,1)S(1)}, u32[]{:S(2)}) copy-start(bf16[128,1152]{1,0:T(8,128)(2,1)S(1)} %collective-permute-done) | copy-start | bytes 884740
  88.0 10.6 %collective-permute-start.1 = (bf16[2,128,576]{2,1,0:T(8,128)(2,1)S(1)}, bf16[2,128,576]{2,1,0:T(8,128)(2,1)S(1)}, u32[]{:S(2)}, u32[]{:S(2)}) collective-permute-start(bf16[2,128,576]{2,1,0:T(8,128)(2,1)S(1)} %copy.227), channel_id=1, source_target_pairs={{0,16},{16,0},{1,17},{17,1},{2,18},{18,2},{3,19},{19,3},{4,20},{20... | collective-permute-start | bytes 884744 | tf_op jit(solution)/shard_map/ppermute | solution.py:196
  91.0 14.1 %collective-permute-start.2 = (bf16[128,1152]{1,0:T(8,128)(2,1)}, bf16[128,1152]{1,0:T(8,128)(2,1)}, u32[]{:S(2)}, u32[]{:S(2)}) collective-permute-start(bf16[128,1152]{1,0:T(8,128)(2,1)} %fusion.45), channel_id=1, source_target_pairs={{0,16},{16,0},{1,17},{17,1},{2,18},{18,2},{3,19},{19,3},{4,20},{20... | collective-permute-start | bytes 884744 | tf_op jit(solution)/shard_map/ppermute | solution.py:196
  103.3 7.8 %collective-permute-start.3 = (bf16[128,1152]{1,0:T(8,128)(2,1)S(1)}, bf16[128,1152]{1,0:T(8,128)(2,1)S(1)}, u32[]{:S(2)}, u32[]{:S(2)}) collective-permute-start(bf16[128,1152]{1,0:T(8,128)(2,1)S(1)} %add_convert_fusion), channel_id=1, source_target_pairs={{0,16},{16,0},{1,17},{17,1},{2,18},{18,2},{3,19},{19,3},{4,20},{20... | collective-permute-start | bytes 884744 | tf_op jit(solution)/shard_map/ppermute | solution.py:196
  191.5 205.3 %reduce-scatter.7.cloned.1.call-start = ((), (), s32[]{:S(2)}) async-start(), calls=%async_computation.11 | async-start | bytes 5953536
  193.2 69.5 %collective-permute-start.8 = (bf16[72,1728]{1,0:T(8,128)(2,1)}, bf16[72,1728]{1,0:T(8,128)(2,1)}, u32[]{:S(2)}, u32[]{:S(2)}) collective-permute-start(bf16[72,1728]{1,0:T(8,128)(2,1)} %convert_element_type.194), channel_id=1, source_target_pairs={{0,16},{16,0},{1,17},{17,1},{2,18},{18,2},{3,19},{19,3},{4,20},{20... | collective-permute-start | bytes 746504 | tf_op jit(solution)/shard_map/ppermute | solution.py:196
  196.3 58.4 %collective-permute-start.9 = (bf16[72,576]{1,0:T(8,128)(2,1)}, bf16[72,576]{1,0:T(8,128)(2,1)}, u32[]{:S(2)}, u32[]{:S(2)}) collective-permute-start(bf16[72,576]{1,0:T(8,128)(2,1)} %convert_element_type.195), channel_id=1, source_target_pairs={{0,16},{16,0},{1,17},{17,1},{2,18},{18,2},{3,19},{19,3},{4,20},{20... | collective-permute-start | bytes 248840 | tf_op jit(solution)/shard_map/ppermute | solution.py:196
  198.8 66.1 %collective-permute-start.10 = (bf16[72,2304]{1,0:T(8,128)(2,1)}, bf16[72,2304]{1,0:T(8,128)(2,1)}, u32[]{:S(2)}, u32[]{:S(2)}) collective-permute-start(bf16[72,2304]{1,0:T(8,128)(2,1)} %convert_element_type.196), channel_id=1, source_target_pairs={{0,16},{16,0},{1,17},{17,1},{2,18},{18,2},{3,19},{19,3},{4,20},{20... | collective-permute-start | bytes 995336 | tf_op jit(solution)/shard_map/ppermute | solution.py:196
  201.1 94.5 %collective-permute-start.12 = (bf16[432,576]{1,0:T(8,128)(2,1)}, bf16[432,576]{1,0:T(8,128)(2,1)}, u32[]{:S(2)}, u32[]{:S(2)}) collective-permute-start(bf16[432,576]{1,0:T(8,128)(2,1)} %bitcast_convert_fusion.1), channel_id=1, source_target_pairs={{0,16},{16,0},{1,17},{17,1},{2,18},{18,2},{3,19},{19,3},{4,20},{20... | collective-permute-start | bytes 1493000 | tf_op jit(solution)/shard_map/ppermute | solution.py:196
  215.3 13.8 %collective-permute-start.5 = (bf16[128,1152]{1,0:T(8,128)(2,1)S(1)}, bf16[128,1152]{1,0:T(8,128)(2,1)S(1)}, u32[]{:S(2)}, u32[]{:S(2)}) collective-permute-start(bf16[128,1152]{1,0:T(8,128)(2,1)S(1)} %slice.288), channel_id=1, source_target_pairs={{0,16},{16,0},{1,17},{17,1},{2,18},{18,2},{3,19},{19,3},{4,20},{20... | collective-permute-start | bytes 884744 | tf_op jit(solution)/shard_map/ppermute | solution.py:196
  222.5 15.0 %copy-start.23 = (bf16[1,128,1152]{2,1,0:T(8,128)(2,1)S(1)}, bf16[1,128,1152]{2,1,0:T(8,128)(2,1)}, u32[]{:S(2)}) copy-start(bf16[1,128,1152]{2,1,0:T(8,128)(2,1)} %param.25) | copy-start | bytes 884740
  222.5 15.0 %copy-start.43 = (f32[128,1152]{1,0:T(8,128)S(1)}, f32[128,1152]{1,0:T(8,128)}, u32[]{:S(2)}) copy-start(f32[128,1152]{1,0:T(8,128)} %get-tuple-element.166) | copy-start | bytes 1769476
  222.5 15.0 %copy-start.53 = (f32[1152]{0:T(1024)S(1)}, f32[1152]{0:T(1024)}, u32[]{:S(2)}) copy-start(f32[1152]{0:T(1024)} %get-tuple-element.112) | copy-start | bytes 13828
  222.5 15.0 %copy-start.54 = (f32[1152]{0:T(1024)S(1)}, f32[1152]{0:T(1024)}, u32[]{:S(2)}) copy-start(f32[1152]{0:T(1024)} %get-tuple-element.107) | copy-start | bytes 13828
  222.5 15.0 %copy-start.63 = (f32[1152]{0:T(1024)S(1)}, f32[1152]{0:T(1024)}, u32[]{:S(2)}) copy-start(f32[1152]{0:T(1024)} %get-tuple-element.146) | copy-start | bytes 13828
  229.1 8.4 %collective-permute-start.4 = (bf16[128,1152]{1,0:T(8,128)(2,1)S(1)}, bf16[128,1152]{1,0:T(8,128)(2,1)S(1)}, u32[]{:S(2)}, u32[]{:S(2)}) collective-permute-start(bf16[128,1152]{1,0:T(8,128)(2,1)S(1)} %slice.289), channel_id=1, source_target_pairs={{0,16},{16,0},{1,17},{17,1},{2,18},{18,2},{3,19},{19,3},{4,20},{20... | collective-permute-start | bytes 884744 | tf_op jit(solution)/shard_map/ppermute | solution.py:196
  239.7 7.8 %collective-permute-start.6 = (bf16[128,1152]{1,0:T(8,128)(2,1)S(1)}, bf16[128,1152]{1,0:T(8,128)(2,1)S(1)}, u32[]{:S(2)}, u32[]{:S(2)}) collective-permute-start(bf16[128,1152]{1,0:T(8,128)(2,1)S(1)} %multiply_convert_fusion.2), channel_id=1, source_target_pairs={{0,16},{16,0},{1,17},{17,1},{2,18},{18,2},{3,19},{19,3},{4,20},{20... | collective-permute-start | bytes 884744 | tf_op jit(solution)/shard_map/ppermute | solution.py:196
  247.4 8.1 %collective-permute-start.14 = (bf16[72,576]{1,0:T(8,128)(2,1)}, bf16[72,576]{1,0:T(8,128)(2,1)}, u32[]{:S(2)}, u32[]{:S(2)}) collective-permute-start(bf16[72,576]{1,0:T(8,128)(2,1)} %convert_element_type.200), channel_id=1, source_target_pairs={{0,16},{16,0},{1,17},{17,1},{2,18},{18,2},{3,19},{19,3},{4,20},{20... | collective-permute-start | bytes 248840 | tf_op jit(solution)/shard_map/ppermute | solution.py:196
  254.7 9.4 %collective-permute-start.13 = (bf16[72,1728]{1,0:T(8,128)(2,1)}, bf16[72,1728]{1,0:T(8,128)(2,1)}, u32[]{:S(2)}, u32[]{:S(2)}) collective-permute-start(bf16[72,1728]{1,0:T(8,128)(2,1)} %convert_element_type.199), channel_id=1, source_target_pairs={{0,16},{16,0},{1,17},{17,1},{2,18},{18,2},{3,19},{19,3},{4,20},{20... | collective-permute-start | bytes 746504 | tf_op jit(solution)/shard_map/ppermute | solution.py:196
  255.5 40.2 %collective-permute-start.17 = (bf16[432,576]{1,0:T(8,128)(2,1)}, bf16[432,576]{1,0:T(8,128)(2,1)}, u32[]{:S(2)}, u32[]{:S(2)}) collective-permute-start(bf16[432,576]{1,0:T(8,128)(2,1)} %bitcast_convert_fusion), channel_id=1, source_target_pairs={{0,16},{16,0},{1,17},{17,1},{2,18},{18,2},{3,19},{19,3},{4,20},{20... | collective-permute-start | bytes 1493000 | tf_op jit(solution)/shard_map/ppermute | solution.py:196
  262.7 21.2 %collective-permute-start.11 = (bf16[288,576]{1,0:T(8,128)(2,1)}, bf16[288,576]{1,0:T(8,128)(2,1)}, u32[]{:S(2)}, u32[]{:S(2)}) collective-permute-start(bf16[288,576]{1,0:T(8,128)(2,1)} %convert_element_type.197), channel_id=1, source_target_pairs={{0,16},{16,0},{1,17},{17,1},{2,18},{18,2},{3,19},{19,3},{4,20},{20... | collective-permute-start | bytes 995336 | tf_op jit(solution)/shard_map/ppermute | solution.py:196
  264.1 26.9 %collective-permute-start.15 = (bf16[72,2304]{1,0:T(8,128)(2,1)}, bf16[72,2304]{1,0:T(8,128)(2,1)}, u32[]{:S(2)}, u32[]{:S(2)}) collective-permute-start(bf16[72,2304]{1,0:T(8,128)(2,1)} %convert_element_type.201), channel_id=1, source_target_pairs={{0,16},{16,0},{1,17},{17,1},{2,18},{18,2},{3,19},{19,3},{4,20},{20... | collective-permute-start | bytes 995336 | tf_op jit(solution)/shard_map/ppermute | solution.py:196
  264.9 30.8 %collective-permute-start.16 = (bf16[288,576]{1,0:T(8,128)(2,1)}, bf16[288,576]{1,0:T(8,128)(2,1)}, u32[]{:S(2)}, u32[]{:S(2)}) collective-permute-start(bf16[288,576]{1,0:T(8,128)(2,1)} %convert_element_type.202), channel_id=1, source_target_pairs={{0,16},{16,0},{1,17},{17,1},{2,18},{18,2},{3,19},{19,3},{4,20},{20... | collective-permute-start | bytes 995336 | tf_op jit(solution)/shard_map/ppermute | solution.py:196
  281.6 29.0 %copy-start.69 = (f32[1152]{0:T(1024)S(1)}, f32[1152]{0:T(1024)}, u32[]{:S(2)}) copy-start(f32[1152]{0:T(1024)} %get-tuple-element.131) | copy-start | bytes 13828
  281.6 29.1 %copy-start.68 = (f32[1152]{0:T(1024)S(1)}, f32[1152]{0:T(1024)}, u32[]{:S(2)}) copy-start(f32[1152]{0:T(1024)} %get-tuple-element.129) | copy-start | bytes 13828
  311.1 12.8 %copy-start.62 = (f32[1152]{0:T(1024)S(1)}, f32[1152]{0:T(1024)}, u32[]{:S(2)}) copy-start(f32[1152]{0:T(1024)} %get-tuple-element.134) | copy-start | bytes 13828
  311.1 15.4 %copy-start.61 = (f32[1152]{0:T(1024)S(1)}, f32[1152]{0:T(1024)}, u32[]{:S(2)}) copy-start(f32[1152]{0:T(1024)} %get-tuple-element.105) | copy-start | bytes 13828
  316.0 16.5 %copy-start.60 = (f32[1152]{0:T(1024)S(1)}, f32[1152]{0:T(1024)}, u32[]{:S(2)}) copy-start(f32[1152]{0:T(1024)} %get-tuple-element.133) | copy-start | bytes 13828
  316.0 17.9 %copy-start.59 = (f32[1152]{0:T(1024)S(1)}, f32[1152]{0:T(1024)}, u32[]{:S(2)}) copy-start(f32[1152]{0:T(1024)} %get-tuple-element.101) | copy-start | bytes 13828
  316.0 11.8 %collective-permute-start.7 = (bf16[128,1152]{1,0:T(8,128)(2,1)S(1)}, bf16[128,1152]{1,0:T(8,128)(2,1)S(1)}, u32[]{:S(2)}, u32[]{:S(2)}) collective-permute-start(bf16[128,1152]{1,0:T(8,128)(2,1)S(1)} %slice.287), channel_id=1, source_target_pairs={{0,16},{16,0},{1,17},{17,1},{2,18},{18,2},{3,19},{19,3},{4,20},{20... | collective-permute-start | bytes 884744 | tf_op jit(solution)/shard_map/ppermute | solution.py:196
  327.8 15.5 %copy-start.34 = (bf16[128,1152]{1,0:T(8,128)(2,1)}, bf16[128,1152]{1,0:T(8,128)(2,1)S(1)}, u32[]{:S(2)}) copy-start(bf16[128,1152]{1,0:T(8,128)(2,1)S(1)} %collective-permute-done.7) | copy-start | bytes 884740
  339.8 11.1 %all-to-all-start.2 = ((bf16[32,2,216]{2,1,0:T(2,128)(2,1)}), bf16[32,2,216]{2,1,0:T(2,128)(2,1)}, u32[]{:S(2)}, u32[]{:S(2)}) async-start(bf16[32,2,216]{2,1,0:T(2,128)(2,1)} %reshape.316), calls=%async_computation.2 | async-start | bytes 65536 | tf_op jit(solution)/shard_map/all_to_all | solution.py:366
  351.0 11.1 %all-to-all-start.4 = ((f32[32,1,504]{2,1,0:T(1,128)}), f32[32,1,504]{2,1,0:T(1,128)}, u32[]{:S(2)}, u32[]{:S(2)}) async-start(f32[32,1,504]{2,1,0:T(1,128)} %all_to_all.52), calls=%async_computation.4 | async-start | bytes 131072 | tf_op jit(solution)/shard_map/all_to_all | solution.py:390
  355.8 21.3 %collective-permute-start.18 = (bf16[72,4608]{1,0:T(8,128)(2,1)S(1)}, bf16[72,4608]{1,0:T(8,128)(2,1)S(1)}, u32[]{:S(2)}, u32[]{:S(2)}) collective-permute-start(bf16[72,4608]{1,0:T(8,128)(2,1)S(1)} %copy-done.11), channel_id=1, source_target_pairs={{0,16},{16,0},{1,17},{17,1},{2,18},{18,2},{3,19},{19,3},{4,20},{20... | collective-permute-start | bytes 1990664 | tf_op jit(solution)/shard_map/ppermute | solution.py:196
  362.0 12.2 %all-to-all-start.3 = ((f32[16,1,1152]{2,1,0:T(1,128)}), f32[16,1,1152]{2,1,0:T(1,128)S(1)}, u32[]{:S(2)}, u32[]{:S(2)}) async-start(f32[16,1,1152]{2,1,0:T(1,128)} %copy.249), calls=%async_computation.3 | async-start | bytes 147456 | tf_op jit(solution)/shard_map/all_to_all | solution.py:372
  385.4 17.9 %copy-start.64 = (f32[1,1152]{1,0:T(1,128)S(1)}, f32[1,1152]{1,0:T(1,128)}, u32[]{:S(2)}) copy-start(f32[1,1152]{1,0:T(1,128)} %get-tuple-element.122) | copy-start | bytes 13828
  385.4 17.9 %copy-start.65 = (f32[1,1152]{1,0:T(1,128)S(1)}, f32[1,1152]{1,0:T(1,128)}, u32[]{:S(2)}) copy-start(f32[1,1152]{1,0:T(1,128)} %get-tuple-element.123) | copy-start | bytes 13828
  399.9 10.9 %all-to-all-start.5 = ((f32[32,1,505]{2,1,0:T(1,128)}), f32[32,1,505]{2,1,0:T(1,128)S(1)}, u32[]{:S(2)}, u32[]{:S(2)}) async-start(f32[32,1,505]{2,1,0:T(1,128)} %broadcast_in_dim.118), calls=%async_computation.6 | async-start | bytes 131072 | tf_op jit(solution)/shard_map/all_to_all | solution.py:209
  403.9 28.8 %collective-permute-start.19 = (bf16[72,2368]{1,0:T(8,128)(2,1)}, bf16[72,2368]{1,0:T(8,128)(2,1)S(1)}, u32[]{:S(2)}, u32[]{:S(2)}) collective-permute-start(bf16[72,2368]{1,0:T(8,128)(2,1)} %reduce-scatter.7.cloned.1.call-done.refs_0_), channel_id=1, source_target_pairs={{0,16},{16,0},{1,17},{17,1},{2,18},{18,2},{3,19},{19,3},{4,20},{20... | collective-permute-start | bytes 1022984 | tf_op jit(solution)/shard_map/ppermute | solution.py:196
  (64 other events, 286.9 us)
Sparse Core Ops, SparseCore 0:
  10.7 68.6 all-gather.2
  82.3 87.0 all-gather.4
  191.6 118.9 reduce-scatter.4
  314.4 82.2 reduce-scatter.6

commit v3 on v2

--- a/solution.py
+++ b/solution.py
@@ -134,8 +134,8 @@
                     second_new = (
                         beta_two * second_old.astype(jnp.float32) + (1.0 - beta_two) * grad * grad
                     )
-                    first_hat = first_new / (1.0 - beta_one**step_count)
-                    second_hat = second_new / (1.0 - beta_two**step_count)
+                    first_hat = first_new * (1.0 / (1.0 - beta_one**step_count))
+                    second_hat = second_new * (1.0 / (1.0 - beta_two**step_count))
                     old = cut(w_ref, w_at)
                     change = -learn_rate * (
                         first_hat / (jnp.sqrt(second_hat) + adam_eps) + decay_rate * old
@@ -220,21 +220,26 @@
     b_one = jnp.transpose(units, (1, 0, 2)).reshape(folds, width)
 
     wq_half = own_half(w_qkv.astype(jnp.bfloat16).reshape(rows, 3, inner), 2)
-    pack_attn = jnp.concatenate(
-        [w_proj.astype(jnp.bfloat16), wq_half.reshape(rows, 3 * half)], axis=1
-    )
-    full_attn = lax.all_gather(pack_attn, "shard", axis=0, tiled=True)
-    wp_b = full_attn[:, :width]
-    wq_b = full_attn[:, width:]
     w1_half = lax.dynamic_index_in_dim(
         w_fc1.astype(jnp.bfloat16).reshape(rows, parts, 2, folds, unit), turn, 2, keepdims=False
     )
     w1_half = jnp.transpose(w1_half, (0, 2, 1, 3)).reshape(rows, folds * width)
+    pack_first = jnp.concatenate(
+        [w_proj.astype(jnp.bfloat16), w1_half, wq_half.reshape(rows, 3 * half)], axis=1
+    )
+    full_first = lax.all_gather(pack_first, "shard", axis=0, tiled=True)
     w2_half = own_half(w_fc2.astype(jnp.bfloat16), 0).reshape(folds, rows, width)
-    pack_mlp = jnp.concatenate([w1_half] + [w2_half[f] for f in range(folds)], axis=1)
-    full_mlp = lax.all_gather(pack_mlp, "shard", axis=0, tiled=True)
-    w1_b = [full_mlp[:, f * width : (f + 1) * width] for f in range(folds)]
-    w2_b = [full_mlp[:, (folds + f) * width : (folds + f + 1) * width] for f in range(folds)]
+    pack_second = jnp.concatenate([w2_half[f] for f in range(folds)], axis=1)
+    full_second = lax.all_gather(pack_second, "shard", axis=0, tiled=True)
+    firsts = (m_qkv, m_proj, m_fc1, m_fc2, m_ada.T)
+    seconds = (v_qkv, v_proj, v_fc1, v_fc2, v_ada.T)
+    fars = []
+    if replicas == 2:
+        fars = [swap(value.astype(jnp.bfloat16)) for value in firsts + seconds]
+    full_first, fars = lax.optimization_barrier((full_first, fars))
+    wp_b = full_first[:, :width]
+    w1_b = [full_first[:, (1 + f) * width : (2 + f) * width] for f in range(folds)]
+    wq_b = full_first[:, (1 + folds) * width :]
 
     cvec = cond + time_embed(timesteps, width)
     silu_c = jax.nn.silu(cvec).astype(jnp.bfloat16)
@@ -277,40 +282,30 @@
     a_two = (n_two * (1.0 + scale2) + shift2).astype(jnp.bfloat16)
     a_two2 = jnp.concatenate([a_two, swap(a_two)], axis=0)
 
-    g_one = []
-    g_two = []
-    g_b_one = []
+    acts = []
+    slopes = []
     for f in range(folds):
         pre = product("ld,df->lf", a_two2, w1_b[f]) + b_one[f]
         act_val, act_slope = gelu_parts(pre)
-        act = act_val.astype(jnp.bfloat16)
-        d_pre = product("ld,fd->lf", d_mlp2, w2_b[f]) * act_slope
+        acts.append(act_val.astype(jnp.bfloat16))
+        slopes.append(act_slope)
+    pack_two = pack_products(
+        (acts, [d_mlp2]), [[(f, 0, 0)] for f in range(folds)], "pack_two", folds * width, width
+    )
+    grads_two = lax.psum_scatter(pack_two, "shard", scatter_dimension=0, tiled=True)
+    full_second, slopes, pack_two = lax.optimization_barrier((full_second, slopes, pack_two))
+    w2_b = [full_second[:, f * width : (f + 1) * width] for f in range(folds)]
+    d_a2_sum = 0.0
+    d_pres = []
+    g_b_one = []
+    for f in range(folds):
+        d_pre = product("ld,fd->lf", d_mlp2, w2_b[f]) * slopes[f]
         d_pre_b = d_pre.astype(jnp.bfloat16)
-        g_one.append(d_pre_b)
-        g_two.append(act)
+        d_a2_sum = d_a2_sum + product("lf,df->ld", d_pre_b, w1_b[f])
+        d_pres.append(d_pre_b)
         g_b_one.append(jnp.sum(d_pre, axis=0))
-    picks = [[(0, f, 0)] for f in range(folds)] + [[(1 + f, folds, 0)] for f in range(folds)]
-    pack_mlp_grad = pack_products(
-        ([a_two2] + g_two, g_one + [d_mlp2]), picks, "pack_mlp", 2 * folds * width, width
-    )
-    g_one, g_two, pack_mlp_grad = lax.optimization_barrier((g_one, g_two, pack_mlp_grad))
-    mlp_sum = 0.0
-    d_a2_sum = 0.0
-    for f in range(folds):
-        d_a2_sum = d_a2_sum + product("lf,df->ld", g_one[f], w1_b[f])
-        mlp_sum = mlp_sum + product("lf,fd->ld", g_two[f], w2_b[f])
     d_a2_far = swap(d_a2_sum[length:].astype(jnp.bfloat16))
-    grads_mlp = lax.psum_scatter(pack_mlp_grad, "shard", scatter_dimension=0, tiled=True)
     d_a2 = d_a2_sum[:length] + d_a2_far.astype(jnp.float32)
-    mlp = (
-        mlp_sum[:length]
-        + swap(mlp_sum[length:].astype(jnp.bfloat16)).astype(jnp.float32)
-        + b_fc2
-    )
-    block_out = (x_one + gate2 * mlp)[None]
-    d_gate2 = jnp.sum(grad_out * mlp, axis=0)
-    g_b_fc2 = jnp.sum(d_mlp, axis=0)
-
     d_shift2 = jnp.sum(d_a2, axis=0)
     d_scale2 = jnp.sum(d_a2 * n_two, axis=0)
     dx_one = grad_out + norm_back(d_a2 * (1.0 + scale2), n_two, r_two)
@@ -340,20 +335,32 @@
     )
     proj_wide = -(-half // 128) * 128
     d_attn_half = jnp.pad(own_half(d_attn2, 1), ((0, 0), (0, proj_wide - half)))
-    pack_attn_grad = pack_products(
-        ([heads_all, a_one2], [d_attn_half, d_qkv]),
-        [[(0, 0, 0), (1, 1, proj_wide)]],
-        "pack_attn",
-        proj_wide + 3 * half,
+    one_wide = folds * width
+    picks = [(0, f, f * width) for f in range(folds)]
+    picks += [(1, folds, one_wide), (2, folds + 1, one_wide + proj_wide)]
+    pack_rest = pack_products(
+        ([a_two2, heads_all, a_one2], d_pres + [d_attn_half, d_qkv]),
+        [picks],
+        "pack_rest",
+        one_wide + proj_wide + 3 * half,
         3 * 128,
     )
-    firsts = (m_qkv, m_proj, m_fc1, m_fc2, m_ada.T)
-    seconds = (v_qkv, v_proj, v_fc1, v_fc2, v_ada.T)
-    fars = []
-    if replicas == 2:
-        fars = [swap(value.astype(jnp.bfloat16)) for value in firsts + seconds]
-    fars, grads_mlp, pack_attn_grad = lax.optimization_barrier((fars, grads_mlp, pack_attn_grad))
-    grads_attn = lax.psum_scatter(pack_attn_grad, "shard", scatter_dimension=0, tiled=True)
+    grads_two, pack_rest, acts, d_qkv = lax.optimization_barrier(
+        (grads_two, pack_rest, acts, d_qkv)
+    )
+    grads_rest = lax.psum_scatter(pack_rest, "shard", scatter_dimension=0, tiled=True)
+    mlp_sum = 0.0
+    for f in range(folds):
+        mlp_sum = mlp_sum + product("lf,fd->ld", acts[f], w2_b[f])
+    mlp = (
+        mlp_sum[:length]
+        + swap(mlp_sum[length:].astype(jnp.bfloat16)).astype(jnp.float32)
+        + b_fc2
+    )
+    block_out = (x_one + gate2 * mlp)[None]
+    d_gate2 = jnp.sum(grad_out * mlp, axis=0)
+    g_b_fc2 = jnp.sum(d_mlp, axis=0)
+
     d_a1_sum = product("le,de->ld", d_qkv, wq_b)
     d_a1 = d_a1_sum[:length] + swap(d_a1_sum[length:].astype(jnp.bfloat16)).astype(jnp.float32)
     d_shift1 = jnp.sum(d_a1, axis=0)
@@ -394,22 +401,28 @@
 
     count_ada = width // replicas
     own_ada = lax.dynamic_slice_in_dim(g_ada, rank * count_ada, count_ada, 1)
-    far_mlp = swap(grads_mlp) if replicas == 2 else jnp.zeros_like(grads_mlp)
-    both_mlp = jnp.where(turn == 0, jnp.stack([grads_mlp, far_mlp]), jnp.stack([far_mlp, grads_mlp]))
-    full_one = both_mlp[:, :, : folds * width].reshape(2, rows, folds, parts, unit)
-    full_one = jnp.transpose(full_one, (1, 3, 0, 2, 4)).reshape(rows, FF)
-    full_two = both_mlp[:, :, folds * width :].reshape(2, rows, folds, width)
+    def pair_of(own, far):
+        return jnp.where(turn == 0, jnp.stack([own, far]), jnp.stack([far, own]))
+
+    def full_of_one(own, far):
+        full = pair_of(own, far).reshape(2, rows, folds, parts, unit)
+        return jnp.transpose(full, (1, 3, 0, 2, 4)).reshape(rows, FF)
+
+    far_two = swap(grads_two) if replicas == 2 else jnp.zeros_like(grads_two)
+    full_two = pair_of(grads_two, far_two).reshape(2, rows, folds, width)
     full_two = jnp.transpose(full_two, (0, 2, 1, 3)).reshape(2 * folds * rows, width)
 
     weights = (w_qkv, w_proj, w_fc1, w_fc2, w_ada.T)
     if replicas == 2:
-        early = sum((jnp.sum(jnp.square(g.astype(jnp.float32))) for g in (grads_mlp, own_ada)))
+        early = sum((jnp.sum(jnp.square(g.astype(jnp.float32))) for g in (grads_two, own_ada)))
         early = early + jnp.sum(bias_chunk * bias_chunk)
-        grads_attn, full_one, full_two, g_ada, early = lax.optimization_barrier(
-            (grads_attn, full_one, full_two, g_ada, early)
+        grads_rest, full_two, g_ada, early = lax.optimization_barrier(
+            (grads_rest, full_two, g_ada, early)
         )
-        counted = [grads_attn.astype(jnp.float32)]
+        counted = [grads_rest.astype(jnp.float32)]
     else:
+        grads_attn = grads_rest[:, one_wide:]
+        full_one = full_of_one(grads_rest[:, :one_wide], jnp.zeros_like(grads_two))
         blank = jnp.zeros_like(grads_attn)
         both = ordered(grads_attn[None], blank[None], 0)
         full_proj = jnp.transpose(both[:, :, :half], (1, 0, 2)).reshape(rows, inner)
@@ -431,19 +444,21 @@
     new_m = []
     new_v = []
     if replicas == 2:
-        far_attn = swap(grads_attn)
+        far_rest = swap(grads_rest)
+        full_one = full_of_one(grads_rest[:, :one_wide], far_rest[:, :one_wide])
         scalars = (clip.reshape(1), turn.reshape(1).astype(jnp.int32))
-        pair_attn = (grads_attn, far_attn)
+        qkv_at = one_wide + proj_wide
+        pair_attn = (grads_rest, far_rest)
         sources = (pair_attn, pair_attn, (full_one,), (full_two,), (g_ada,))
         plans = (
             (
                 half,
                 [
-                    (half * b, b % 2, proj_wide + half * (b // 2), b // 3, half * (b % 3))
+                    (half * b, b % 2, qkv_at + half * (b // 2), b // 3, half * (b % 3))
                     for b in range(6)
                 ],
             ),
-            (half, [(half * b, b, 0, b, 0) for b in range(2)]),
+            (half, [(half * b, b, one_wide, b, 0) for b in range(2)]),
             (FF // 2, [(FF // 2 * b, -1, FF // 2 * b, b, 0) for b in range(2)]),
             (half, [(half * b, -1, half * b, b, 0) for b in range(2)]),
             (count_ada, [(count_ada * b, -1, count_ada * b, b, 0) for b in range(2)]),

time: 455 us -> 452 us (level)
  waiting for transfers between devices: 185 us -> 148 us
  local copies, waits for them, and re-layouts: 53.1 us -> 73.4 us
  other arithmetic: 48.7 us -> 54.3 us
  matrix products: 50.7 us -> 55.7 us
    all_gather x2, waiting for transfers between devices: 78.7 us -> 19.9 us  [the longest x1 13.3 us: shards(): full_first = lax.all_gather(pack_first, 'shard', axis=0, tiled=True)]
    optimization_barrier x1, waiting for transfers between devices: 10.4 us -> 44.5 us  [shards(): lax.optimization_barrier((grads_rest, full_two, g_ada, early))]
    ppermute x20, waiting for transfers between devices: 49.1 us -> 64.4 us  [swap(): return lax.ppermute(value, 'rep', couples)]
    all_to_all x2, waiting for transfers between devices: 13.5 us -> 0.29 us  [spread(): return lax.all_to_all(copies, axes, split_axis=0, concat_axis=0, tiled=True)]
    reduce_scatter x1, waiting for transfers between devices: 14.9 us -> 4.44 us  [shards(): lax.psum_scatter(pack_two, 'shard', scatter_dimension=0, tiled=True)]
    another operation x0 -> x8, local copies, waits for them, and re-layouts: none -> 10.1 us  [pair_of(): return jnp.where(turn == 0, jnp.stack([own, far]), jnp.stack([far, own]))]
    all_to_all x1, waiting for transfers between devices: 6.2 us -> 0.42 us  [shards(): lax.all_to_all(mod_cols, 'shard', split_axis=0, concat_axis=1, tiled=True)]
    reshape x6, local copies, waits for them, and re-layouts: 7.06 us -> 12.7 us  [shards(): piece.astype(jnp.bfloat16).reshape(2 * length, half)]
  transfers between devices with their start and end apart: 30 -> 30, of which waited for: 20 -> 18; matrix products, arithmetic and copies ran while one was open for 28% -> 36% of each run, Pallas kernels for 6% -> 6%
where the time goes in v3:
time: 452 us; the launch traced here: 444 us
  waiting for transfers between devices  148 us (33%)
  local copies, waits for them, and re-layouts  73.4 us (16%)
  matrix products  55.7 us (12%)
  other arithmetic  54.3 us (12%)
  starting transfers between devices  52.7 us (12%)
  Pallas kernels  40.3 us (9%)
  between operations  19.1 us (4%)
    ppermute x20, waiting for transfers between devices, swap(): return lax.ppermute(value, 'rep', couples)  64.4 us
    dot_general x17, matrix products, product(): return jnp.einsum(form, left, right, preferred_element_type=jnp.float32)  52.1 us
    optimization_barrier x1, waiting for transfers between devices, shards(): lax.optimization_barrier((grads_rest, full_two, g_ada, early))  44.5 us
    pallas_call x5, Pallas kernels, update_both(): pl.pallas_call(body, in_specs=[smem, smem] + [vmem] * (5 + len(grads)), o...  27.2 us
    ppermute x20, starting transfers between devices, swap(): return lax.ppermute(value, 'rep', couples)  23.4 us
    unnamed x157, local copies, waits for them, and re-layouts  15.8 us
    all_gather x1, waiting for transfers between devices, shards(): full_first = lax.all_gather(pack_first, 'shard', axis=0, tiled=True)  13.3 us
    pallas_call x2, Pallas kernels, pack_products(): pl.pallas_call(body, grid=(len(picks), width // block), in_specs=[pl.Bloc...  13.2 us
  transfers between devices with their start and end apart: 30, of which 18 were waited for; matrix products, arithmetic and copies ran while one was open for 36% of the time, Pallas kernels for 6%

profile of v3, /device:TPU:0, one launch (start us, length us, event | category | flops | bytes accessed | tf_op | source)
XLA Modules:
  0.0 444.0 jit_solution(13007910038708935071)
XLA Ops:
  9.9 2.6 reshape.282
  21.0 7.3 %all-to-all-start = ((bf16[32,2,576]{2,1,0:T(2,128)(2,1)}), bf16[32,2,576]{2,1,0:T(2,128)(2,1)S(1)}, u32[]{:S(2)}, u32[]{:S(2)}) async-start(bf16[32,2,576]{2,1,0:T(2,128)(2,1)} %reshape.324), calls=%async_computation | async-start | bytes 163840 | tf_op jit(solution)/shard_map/all_to_all | solution.py:209
  41.7 5.7 %all-to-all-start.1 = ((f32[16,1,432]{2,1,0:T(1,128)}), f32[16,1,432]{2,1,0:T(1,128)}, u32[]{:S(2)}, u32[]{:S(2)}) async-start(f32[16,1,432]{2,1,0:T(1,128)} %copy.258), calls=%async_computation.1 | async-start | bytes 65536 | tf_op jit(solution)/shard_map/all_to_all | solution.py:250
  59.8 17.6 %collective-permute-done.6.refs_5_ = bf16[72,1728]{1,0:T(8,128)(2,1)S(1)} collective-permute-done((bf16[72,1728]{1,0:T(8,128)(2,1)}, bf16[72,1728]{1,0:T(8,128)(2,1)S(1)}, u32[]{:S(2)}, u32[]{:S(2)}) %collective-permute-start.6) | collective-permute-done | bytes 248864 | tf_op jit(solution)/shard_map/ppermute | solution.py:196
  80.7 15.7 %collective-permute-done.8.refs_4_ = bf16[72,2304]{1,0:T(8,128)(2,1)} collective-permute-done((bf16[72,2304]{1,0:T(8,128)(2,1)}, bf16[72,2304]{1,0:T(8,128)(2,1)}, u32[]{:S(2)}, u32[]{:S(2)}) %collective-permute-start.8) | collective-permute-done | bytes 331808 | tf_op jit(solution)/shard_map/ppermute | solution.py:196
  96.5 7.9 %collective-permute-done.9.refs_4_ = bf16[288,576]{1,0:T(8,128)(2,1)} collective-permute-done((bf16[288,576]{1,0:T(8,128)(2,1)}, bf16[288,576]{1,0:T(8,128)(2,1)}, u32[]{:S(2)}, u32[]{:S(2)}) %collective-permute-start.9) | collective-permute-done | bytes 331808 | tf_op jit(solution)/shard_map/ppermute | solution.py:196
  104.4 13.3 %all-gather.3.cloned.1.call-done = bf16[1152,5184]{1,0:T(8,128)(2,1)} async-done(((bf16[72,5184]{1,0:T(8,128)(2,1)}), bf16[1152,5184]{1,0:T(8,128)(2,1)}) %all-gather.3.cloned.1.call-update) | async-done | bytes 11943952 | tf_op jit(solution)/shard_map/all_gather | solution.py:230
  117.7 4.1 fusion.3
  123.7 2.5 fusion.109
  132.8 6.9 %collective-permute-done.11 = bf16[2,128,576]{2,1,0:T(8,128)(2,1)} collective-permute-done((bf16[2,128,576]{2,1,0:T(8,128)(2,1)}, bf16[2,128,576]{2,1,0:T(8,128)(2,1)}, u32[]{:S(2)}, u32[]{:S(2)}) %collective-permute-start.11) | collective-permute-done | bytes 294944 | tf_op jit(solution)/shard_map/ppermute | solution.py:196
  141.7 3.3 fusion.100
  149.7 4.3 collective-permute-done.12
  154.0 4.6 %fusion.31 = (f32[256,1152]{1,0:T(8,128)}, bf16[256,1152]{1,0:T(8,128)(2,1)}) fusion(f32[1152]{0:T(1024)S(1)} %add.248, bf16[1152,5184]{1,0:T(8,128)(2,1)} %all-gather.3.cloned.1.call-done, bf16[128,1152]{1,0:T(8,128)(2,1)} %collective-permute-done.12, bf16[128,1152]{1,0:T(8,128)(2,1)} %add_convert_fusion), kind=kOutput, calls=%fused_computation.49 | convolution fusion | flops 686555136 | bytes 5018112 | tf_op jit(solution)/shard_map/ld,df->lf/dot_general | solution.py:26
  158.6 4.6 %fusion.34 = (f32[256,1152]{1,0:T(8,128)}, bf16[256,1152]{1,0:T(8,128)(2,1)}) fusion(f32[1152]{0:T(1024)S(1)} %add.253, bf16[1152,5184]{1,0:T(8,128)(2,1)} %all-gather.3.cloned.1.call-done, bf16[128,1152]{1,0:T(8,128)(2,1)} %collective-permute-done.12, bf16[128,1152]{1,0:T(8,128)(2,1)} %add_convert_fusion), kind=kOutput, calls=%fused_computation.52 | convolution fusion | flops 686555136 | bytes 5018112 | tf_op jit(solution)/shard_map/ld,df->lf/dot_general | solution.py:26
  163.2 5.0 %pack_two.1 = bf16[1152,2304]{1,0:T(8,128)(2,1)} custom-call(bf16[256,1152]{1,0:T(8,128)(2,1)} %get-tuple-element.63.refs_0_, bf16[256,1152]{1,0:T(8,128)(2,1)} %get-tuple-element.64.refs_1_, bf16[256,1152]{1,0:T(8,128)(2,1)} %pad_maximum_fusion.5.refs_2_), custom_call_target="tpu_custom_call" | custom-call | tf_op jit(solution)/shard_map/pack_two/pallas_call | solution.py:93
  168.4 6.6 %all-gather.5.cloned.1.call-done = bf16[1152,2304]{1,0:T(8,128)(2,1)} async-done(((bf16[72,2304]{1,0:T(8,128)(2,1)}), bf16[1152,2304]{1,0:T(8,128)(2,1)}) %all-gather.5.cloned.1.call-update) | async-done | bytes 5308432 | tf_op jit(solution)/shard_map/all_gather | solution.py:233
  175.0 4.0 fusion.103
  179.8 2.9 fusion.10
  182.7 2.7 fusion.102
  185.4 3.3 convolution_add_fusion.1
  194.1 5.7 %collective-permute-done.14 = bf16[128,1152]{1,0:T(8,128)(2,1)S(1)} collective-permute-done((bf16[128,1152]{1,0:T(8,128)(2,1)}, bf16[128,1152]{1,0:T(8,128)(2,1)S(1)}, u32[]{:S(2)}, u32[]{:S(2)}) %collective-permute-start.14) | collective-permute-done | bytes 294944 | tf_op jit(solution)/shard_map/ppermute | solution.py:196
  207.8 4.0 collective-permute-done.15
  222.5 2.2 reshape.300
  224.7 2.3 fusion.36
  229.1 2.2 reshape.301
  231.3 3.1 fusion.104
  236.4 2.2 reshape.302
  240.7 2.4 concatenate.67.refs_6_
  243.1 8.2 %pack_rest.1 = bf16[1152,4672]{1,0:T(8,128)(2,1)} custom-call(bf16[256,1152]{1,0:T(8,128)(2,1)} %pad_maximum_fusion.4.refs_0_, bf16[256,1152]{1,0:T(8,128)(2,1)} %pad_maximum_fusion.6.refs_1_, bf16[256,1152]{1,0:T(8,128)(2,1)} %pad_maximum_fusion.3.refs_2_, bf16[256,1152]{1,0:T(8,128)(2,1)} %copy-done.20, bf16[256,1152]{1,0:T(8,128)(2,1)} %copy-done.38, ...), custom_call_target="tpu_custom_call" | custom-call | tf_op jit(solution)/shard_map/pack_rest/pallas_call | solution.py:93
  251.3 4.4 reduce-scatter.5.cloned.1.call-done
  263.5 3.1 fusion.7
  266.7 3.1 convolution_add_fusion
  273.4 5.2 %fusion.1 = f32[256,1152]{1,0:T(8,128)} fusion(bf16[256,1728]{1,0:T(8,128)(2,1)S(1)} %copy-done.9, bf16[1152,5184]{1,0:T(8,128)(2,1)} %all-gather.3.cloned.1.call-done), kind=kOutput, calls=%fused_computation.1 | convolution fusion | flops 1019215872 | bytes 6193152 | tf_op jit(solution)/shard_map/le,de->ld/dot_general | solution.py:26
  303.3 3.6 all-to-all-start.2
  308.5 2.3 fusion.53
  314.6 4.2 all-to-all-start.4
  319.9 8.6 %all-to-all-done.4 = f32[32,1,504]{2,1,0:T(1,128)S(1)} async-done(((f32[32,1,504]{2,1,0:T(1,128)}), f32[32,1,504]{2,1,0:T(1,128)S(1)}, u32[]{:S(2)}, u32[]{:S(2)}) %all-to-all-start.4) | async-done | bytes 64544 | tf_op jit(solution)/shard_map/all_to_all | solution.py:397
  328.5 3.5 all-to-all-start.3
  336.3 4.3 all-to-all-done.3
  340.6 44.5 %reduce-scatter.7.cloned.1.call-done.refs_0_ = bf16[72,4672]{1,0:T(8,128)(2,1)} async-done(((bf16[1152,4672]{1,0:T(8,128)(2,1)}), bf16[72,4672]{1,0:T(8,128)(2,1)}) %reduce-scatter.7.cloned.1.call-update) | async-done | bytes 672784 | tf_op jit(solution)/shard_map/optimization_barrier | solution.py:419
  388.5 4.2 all-to-all-start.5
  401.7 5.9 %update.8 = (f32[288,1152]{1,0:T(8,128)}, f32[288,576]{1,0:T(8,128)}, f32[288,576]{1,0:T(8,128)}) custom-call(f32[1]{0:T(128)} %bitcast.32.clip_ref, s32[1]{0:T(128)} %bitcast.33.turn_ref, f32[288,1152]{1,0:T(8,128)} %w_ref.7, bf16[288,1152]{1,0:T(8,128)(2,1)} %bitcast.141, f32[288,576]{1,0:T(8,128)} %refs_1_.3, f32[288,576]{1,0:T(8,128)} %refs_2_.7, ...), custom_call_target="tpu_custom_call" | custom-call | tf_op jit(solution)/shard_map/update/pallas_call | solution.py:147
  407.7 8.7 %update.9 = (f32[432,1152]{1,0:T(8,128)}, f32[432,576]{1,0:T(8,128)}, f32[432,576]{1,0:T(8,128)}) custom-call(f32[1]{0:T(128)} %bitcast.32.clip_ref, s32[1]{0:T(128)} %bitcast.33.turn_ref, f32[432,1152]{1,0:T(8,128)} %bitcast.138, f32[432,1152]{1,0:T(8,128)} %copy-done.1, f32[432,576]{1,0:T(8,128)} %bitcast.139, f32[432,576]{1,0:T(8,128)} %bitcast.140, ...), custom_call_target="tpu_custom_call" | custom-call | tf_op jit(solution)/shard_map/update/pallas_call | solution.py:147
  418.9 2.6 fusion.35
  421.6 3.1 reshape.298.refs_0_
  424.7 5.0 %update.7 = (f32[72,4608]{1,0:T(8,128)}, f32[72,2304]{1,0:T(8,128)}, f32[72,2304]{1,0:T(8,128)}) custom-call(f32[1]{0:T(128)} %bitcast.32.clip_ref, s32[1]{0:T(128)} %bitcast.33.turn_ref, f32[72,4608]{1,0:T(8,128)} %w_ref.6, bf16[72,4608]{1,0:T(8,128)(2,1)} %reshape.298.refs_0_, f32[72,2304]{1,0:T(8,128)} %refs_1_.2, f32[72,2304]{1,0:T(8,128)} %refs_2_.6, ...), custom_call_target="tpu_custom_call" | custom-call | tf_op jit(solution)/shard_map/update/pallas_call | solution.py:147
  429.7 4.7 %update.5 = (f32[72,3456]{1,0:T(8,128)}, f32[72,1728]{1,0:T(8,128)}, f32[72,1728]{1,0:T(8,128)}) custom-call(f32[1]{0:T(128)} %bitcast.32.clip_ref, s32[1]{0:T(128)} %bitcast.33.turn_ref, f32[72,3456]{1,0:T(8,128)} %w_ref.4, bf16[72,4672]{1,0:T(8,128)(2,1)} %reduce-scatter.7.cloned.1.call-done.refs_0_, bf16[72,4672]{1,0:T(8,128)(2,1)} %copy-done.8, ...), custom_call_target="tpu_custom_call" | custom-call | tf_op jit(solution)/shard_map/update/pallas_call | solution.py:147
  434.4 2.9 update.6
  (350 shorter events, 143.6 us)
Async XLA Ops:
  7.2 110.5 %all-gather.3.cloned.1.call-start = ((), (), s32[]{:S(2)}) async-start(), calls=%async_computation.8 | async-start | bytes 12847104 | tf_op jit(solution)/shard_map/all_gather | solution.py:230
  15.0 160.0 %all-gather.5.cloned.1.call-start = ((), (), s32[]{:S(2)}) async-start(), calls=%async_computation.10 | async-start | bytes 5640192 | tf_op jit(solution)/shard_map/all_gather | solution.py:233
  16.2 12.2 %copy-start.22 = (f32[72,1728]{1,0:T(8,128)S(1)}, f32[72,1728]{1,0:T(8,128)}, u32[]{:S(2)}) copy-start(f32[72,1728]{1,0:T(8,128)} %refs_2_.4) | copy-start | bytes 1492996
  16.2 14.6 %copy-start.35 = (f32[72,576]{1,0:T(8,128)S(1)}, f32[72,576]{1,0:T(8,128)}, u32[]{:S(2)}) copy-start(f32[72,576]{1,0:T(8,128)} %refs_2_.5) | copy-start | bytes 497668
  17.0 14.8 %copy-start.17 = (f32[72,2304]{1,0:T(8,128)S(1)}, f32[72,2304]{1,0:T(8,128)}, u32[]{:S(2)}) copy-start(f32[72,2304]{1,0:T(8,128)} %refs_1_.2) | copy-start | bytes 1990660
  20.2 14.1 %copy-start.12 = (f32[288,576]{1,0:T(8,128)S(1)}, f32[288,576]{1,0:T(8,128)}, u32[]{:S(2)}) copy-start(f32[288,576]{1,0:T(8,128)} %refs_1_.3) | copy-start | bytes 1990660
  21.0 18.9 %all-to-all-start = ((bf16[32,2,576]{2,1,0:T(2,128)(2,1)}), bf16[32,2,576]{2,1,0:T(2,128)(2,1)S(1)}, u32[]{:S(2)}, u32[]{:S(2)}) async-start(bf16[32,2,576]{2,1,0:T(2,128)(2,1)} %reshape.324), calls=%async_computation | async-start | bytes 163840 | tf_op jit(solution)/shard_map/all_to_all | solution.py:209
  29.1 29.9 %collective-permute-start.1 = (bf16[72,1728]{1,0:T(8,128)(2,1)}, bf16[72,1728]{1,0:T(8,128)(2,1)}, u32[]{:S(2)}, u32[]{:S(2)}) collective-permute-start(bf16[72,1728]{1,0:T(8,128)(2,1)} %convert_element_type.167), channel_id=1, source_target_pairs={{0,16},{16,0},{1,17},{17,1},{2,18},{18,2},{3,19},{19,3},{4,20},{20... | collective-permute-start | bytes 746504 | tf_op jit(solution)/shard_map/ppermute | solution.py:196
  31.5 24.7 %collective-permute-start.2 = (bf16[72,576]{1,0:T(8,128)(2,1)}, bf16[72,576]{1,0:T(8,128)(2,1)}, u32[]{:S(2)}, u32[]{:S(2)}) collective-permute-start(bf16[72,576]{1,0:T(8,128)(2,1)} %convert_element_type.168), channel_id=1, source_target_pairs={{0,16},{16,0},{1,17},{17,1},{2,18},{18,2},{3,19},{19,3},{4,20},{20... | collective-permute-start | bytes 248840 | tf_op jit(solution)/shard_map/ppermute | solution.py:196
  32.5 45.4 %collective-permute-start.3 = (bf16[72,2304]{1,0:T(8,128)(2,1)}, bf16[72,2304]{1,0:T(8,128)(2,1)}, u32[]{:S(2)}, u32[]{:S(2)}) collective-permute-start(bf16[72,2304]{1,0:T(8,128)(2,1)} %convert_element_type.169), channel_id=1, source_target_pairs={{0,16},{16,0},{1,17},{17,1},{2,18},{18,2},{3,19},{19,3},{4,20},{20... | collective-permute-start | bytes 995336 | tf_op jit(solution)/shard_map/ppermute | solution.py:196
  35.1 44.3 %collective-permute-start.4 = (bf16[288,576]{1,0:T(8,128)(2,1)}, bf16[288,576]{1,0:T(8,128)(2,1)}, u32[]{:S(2)}, u32[]{:S(2)}) collective-permute-start(bf16[288,576]{1,0:T(8,128)(2,1)} %convert_element_type.170), channel_id=1, source_target_pairs={{0,16},{16,0},{1,17},{17,1},{2,18},{18,2},{3,19},{19,3},{4,20},{20... | collective-permute-start | bytes 995336 | tf_op jit(solution)/shard_map/ppermute | solution.py:196
  36.0 21.5 %collective-permute-start.7 = (bf16[72,576]{1,0:T(8,128)(2,1)}, bf16[72,576]{1,0:T(8,128)(2,1)}, u32[]{:S(2)}, u32[]{:S(2)}) collective-permute-start(bf16[72,576]{1,0:T(8,128)(2,1)} %convert_element_type.173), channel_id=1, source_target_pairs={{0,16},{16,0},{1,17},{17,1},{2,18},{18,2},{3,19},{19,3},{4,20},{20... | collective-permute-start | bytes 248840 | tf_op jit(solution)/shard_map/ppermute | solution.py:196
  39.6 19.9 %copy-start.61 = (f32[128]{0:T(128)}, f32[128]{0:T(128)S(1)}, u32[]{:S(2)}) copy-start(f32[128]{0:T(128)S(1)} %broadcast_multiply_fusion.5) | copy-start | bytes 1540
  40.7 10.1 %copy-start.23 = (f32[72,1728]{1,0:T(8,128)S(1)}, f32[72,1728]{1,0:T(8,128)}, u32[]{:S(2)}) copy-start(f32[72,1728]{1,0:T(8,128)} %refs_3_.2) | copy-start | bytes 1492996
  41.1 12.3 %copy-start.13 = (f32[288,576]{1,0:T(8,128)S(1)}, f32[288,576]{1,0:T(8,128)}, u32[]{:S(2)}) copy-start(f32[288,576]{1,0:T(8,128)} %refs_2_.7) | copy-start | bytes 1990660
  41.7 12.9 %all-to-all-start.1 = ((f32[16,1,432]{2,1,0:T(1,128)}), f32[16,1,432]{2,1,0:T(1,128)}, u32[]{:S(2)}, u32[]{:S(2)}) async-start(f32[16,1,432]{2,1,0:T(1,128)} %copy.258), calls=%async_computation.1 | async-start | bytes 65536 | tf_op jit(solution)/shard_map/all_to_all | solution.py:250
  47.4 208.3 %reduce-scatter.5.cloned.1.call-start = ((), (), s32[]{:S(2)}) async-start(), calls=%async_computation.9 | async-start | bytes 5640192 | tf_op jit(solution)/shard_map/reduce_scatter | solution.py:295
  48.0 11.6 %copy-start.64 = (f32[128]{0:T(128)}, f32[128]{0:T(128)S(1)}, u32[]{:S(2)}) copy-start(f32[128]{0:T(128)S(1)} %add_rsqrt_fusion.1) | copy-start | bytes 1540
  53.4 27.3 %copy-start.49 = (f32[16,2,2,72]{3,2,1,0:T(2,128)S(1)}, f32[16,2,2,72]{3,2,1,0:T(2,128)}, u32[]{:S(2)}) copy-start(f32[16,2,2,72]{3,2,1,0:T(2,128)} %reshape.290) | copy-start | bytes 55300
  56.2 48.1 %collective-permute-start.5 = (bf16[432,576]{1,0:T(8,128)(2,1)}, bf16[432,576]{1,0:T(8,128)(2,1)}, u32[]{:S(2)}, u32[]{:S(2)}) collective-permute-start(bf16[432,576]{1,0:T(8,128)(2,1)} %bitcast_convert_fusion.1), channel_id=1, source_target_pairs={{0,16},{16,0},{1,17},{17,1},{2,18},{18,2},{3,19},{19,3},{4,20},{20... | collective-permute-start | bytes 1493000 | tf_op jit(solution)/shard_map/ppermute | solution.py:196
  57.5 19.9 %collective-permute-start.6 = (bf16[72,1728]{1,0:T(8,128)(2,1)}, bf16[72,1728]{1,0:T(8,128)(2,1)S(1)}, u32[]{:S(2)}, u32[]{:S(2)}) collective-permute-start(bf16[72,1728]{1,0:T(8,128)(2,1)} %convert_element_type.172), channel_id=1, source_target_pairs={{0,16},{16,0},{1,17},{17,1},{2,18},{18,2},{3,19},{19,3},{4,20},{20... | collective-permute-start | bytes 746504 | tf_op jit(solution)/shard_map/ppermute | solution.py:196
  59.0 45.4 %collective-permute-start.10 = (bf16[432,576]{1,0:T(8,128)(2,1)}, bf16[432,576]{1,0:T(8,128)(2,1)}, u32[]{:S(2)}, u32[]{:S(2)}) collective-permute-start(bf16[432,576]{1,0:T(8,128)(2,1)} %bitcast_convert_fusion), channel_id=1, source_target_pairs={{0,16},{16,0},{1,17},{17,1},{2,18},{18,2},{3,19},{19,3},{4,20},{20... | collective-permute-start | bytes 1493000 | tf_op jit(solution)/shard_map/ppermute | solution.py:196
  77.4 19.1 %collective-permute-start.8 = (bf16[72,2304]{1,0:T(8,128)(2,1)}, bf16[72,2304]{1,0:T(8,128)(2,1)}, u32[]{:S(2)}, u32[]{:S(2)}) collective-permute-start(bf16[72,2304]{1,0:T(8,128)(2,1)} %convert_element_type.174), channel_id=1, source_target_pairs={{0,16},{16,0},{1,17},{17,1},{2,18},{18,2},{3,19},{19,3},{4,20},{20... | collective-permute-start | bytes 995336 | tf_op jit(solution)/shard_map/ppermute | solution.py:196
  77.9 26.4 %collective-permute-start.9 = (bf16[288,576]{1,0:T(8,128)(2,1)}, bf16[288,576]{1,0:T(8,128)(2,1)}, u32[]{:S(2)}, u32[]{:S(2)}) collective-permute-start(bf16[288,576]{1,0:T(8,128)(2,1)} %convert_element_type.175), channel_id=1, source_target_pairs={{0,16},{16,0},{1,17},{17,1},{2,18},{18,2},{3,19},{19,3},{4,20},{20... | collective-permute-start | bytes 995336 | tf_op jit(solution)/shard_map/ppermute | solution.py:196
  79.4 38.2 %collective-permute-start = (bf16[128,1152]{1,0:T(8,128)(2,1)S(1)}, bf16[128,1152]{1,0:T(8,128)(2,1)S(1)}, u32[]{:S(2)}, u32[]{:S(2)}) collective-permute-start(bf16[128,1152]{1,0:T(8,128)(2,1)S(1)} %fusion.48), channel_id=1, source_target_pairs={{0,16},{16,0},{1,17},{17,1},{2,18},{18,2},{3,19},{19,3},{4,20},{20... | collective-permute-start | bytes 884744 | tf_op jit(solution)/shard_map/ppermute | solution.py:196
  127.9 13.7 %copy-start.18 = (bf16[2,8,72,128]{3,2,1,0:T(8,128)(2,1)}, bf16[2,8,72,128]{3,2,1,0:T(8,128)(2,1)S(1)}, u32[]{:S(2)}) copy-start(bf16[2,8,72,128]{3,2,1,0:T(8,128)(2,1)S(1)} %convolution_convert_fusion.1) | copy-start | bytes 884740
  128.8 10.9 %collective-permute-start.11 = (bf16[2,128,576]{2,1,0:T(8,128)(2,1)}, bf16[2,128,576]{2,1,0:T(8,128)(2,1)}, u32[]{:S(2)}, u32[]{:S(2)}) collective-permute-start(bf16[2,128,576]{2,1,0:T(8,128)(2,1)} %copy.264), channel_id=1, source_target_pairs={{0,16},{16,0},{1,17},{17,1},{2,18},{18,2},{3,19},{19,3},{4,20},{20... | collective-permute-start | bytes 884744 | tf_op jit(solution)/shard_map/ppermute | solution.py:196
  130.4 11.3 %copy-start.60 = (f32[1152]{0:T(1024)S(1)}, f32[1152]{0:T(1024)}, u32[]{:S(2)}) copy-start(f32[1152]{0:T(1024)} %get-tuple-element.148) | copy-start | bytes 13828
  130.4 17.4 %collective-permute-start.13 = (bf16[128,1152]{1,0:T(8,128)(2,1)S(1)}, bf16[128,1152]{1,0:T(8,128)(2,1)}, u32[]{:S(2)}, u32[]{:S(2)}) collective-permute-start(bf16[128,1152]{1,0:T(8,128)(2,1)S(1)} %fusion.46), channel_id=1, source_target_pairs={{0,16},{16,0},{1,17},{17,1},{2,18},{18,2},{3,19},{19,3},{4,20},{20... | collective-permute-start | bytes 884744 | tf_op jit(solution)/shard_map/ppermute | solution.py:196
  146.1 7.9 %collective-permute-start.12 = (bf16[128,1152]{1,0:T(8,128)(2,1)}, bf16[128,1152]{1,0:T(8,128)(2,1)}, u32[]{:S(2)}, u32[]{:S(2)}) collective-permute-start(bf16[128,1152]{1,0:T(8,128)(2,1)} %add_convert_fusion), channel_id=1, source_target_pairs={{0,16},{16,0},{1,17},{17,1},{2,18},{18,2},{3,19},{19,3},{4,20},{20... | collective-permute-start | bytes 884744 | tf_op jit(solution)/shard_map/ppermute | solution.py:196
  168.2 216.9 %reduce-scatter.7.cloned.1.call-start = ((), (), s32[]{:S(2)}) async-start(), calls=%async_computation.11 | async-start | bytes 11593728
  190.4 9.4 %collective-permute-start.14 = (bf16[128,1152]{1,0:T(8,128)(2,1)}, bf16[128,1152]{1,0:T(8,128)(2,1)S(1)}, u32[]{:S(2)}, u32[]{:S(2)}) collective-permute-start(bf16[128,1152]{1,0:T(8,128)(2,1)} %slice.282), channel_id=1, source_target_pairs={{0,16},{16,0},{1,17},{17,1},{2,18},{18,2},{3,19},{19,3},{4,20},{20... | collective-permute-start | bytes 884744 | tf_op jit(solution)/shard_map/ppermute | solution.py:196
  203.4 9.1 %slice-start = ((bf16[1152,5184]{1,0:T(8,128)(2,1)}), bf16[1152,1152]{1,0:T(8,128)(2,1)S(1)}, s32[]{:S(2)}) async-start(bf16[1152,5184]{1,0:T(8,128)(2,1)} %all-gather.3.cloned.1.call-done), calls=%async_computation.12 | async-start | bytes 5308416 | tf_op jit(solution)/shard_map/slice | solution.py:240
  203.4 8.4 %collective-permute-start.15 = (bf16[128,1152]{1,0:T(8,128)(2,1)S(1)}, bf16[128,1152]{1,0:T(8,128)(2,1)S(1)}, u32[]{:S(2)}, u32[]{:S(2)}) collective-permute-start(bf16[128,1152]{1,0:T(8,128)(2,1)S(1)} %multiply_convert_fusion.2), channel_id=1, source_target_pairs={{0,16},{16,0},{1,17},{17,1},{2,18},{18,2},{3,19},{19,3},{4,20},{20... | collective-permute-start | bytes 884744 | tf_op jit(solution)/shard_map/ppermute | solution.py:196
  271.6 15.7 %collective-permute-start.16 = (bf16[128,1152]{1,0:T(8,128)(2,1)}, bf16[128,1152]{1,0:T(8,128)(2,1)}, u32[]{:S(2)}, u32[]{:S(2)}) collective-permute-start(bf16[128,1152]{1,0:T(8,128)(2,1)} %slice.281), channel_id=1, source_target_pairs={{0,16},{16,0},{1,17},{17,1},{2,18},{18,2},{3,19},{19,3},{4,20},{20... | collective-permute-start | bytes 884744 | tf_op jit(solution)/shard_map/ppermute | solution.py:196
  278.6 32.1 %collective-permute-start.18 = (bf16[72,2304]{1,0:T(8,128)(2,1)}, bf16[72,2304]{1,0:T(8,128)(2,1)}, u32[]{:S(2)}, u32[]{:S(2)}) collective-permute-start(bf16[72,2304]{1,0:T(8,128)(2,1)} %reduce-scatter.5.cloned.1.call-done), channel_id=1, source_target_pairs={{0,16},{16,0},{1,17},{17,1},{2,18},{18,2},{3,19},{19,3},{4,20},{20... | collective-permute-start | bytes 995336 | tf_op jit(solution)/shard_map/ppermute | solution.py:196
  281.9 10.3 %collective-permute-start.17 = (bf16[128,1152]{1,0:T(8,128)(2,1)S(1)}, bf16[128,1152]{1,0:T(8,128)(2,1)S(1)}, u32[]{:S(2)}, u32[]{:S(2)}) collective-permute-start(bf16[128,1152]{1,0:T(8,128)(2,1)S(1)} %slice.280), channel_id=1, source_target_pairs={{0,16},{16,0},{1,17},{17,1},{2,18},{18,2},{3,19},{19,3},{4,20},{20... | collective-permute-start | bytes 884744 | tf_op jit(solution)/shard_map/ppermute | solution.py:196
  289.4 19.1 %copy-start.66 = (f32[128]{0:T(128)S(1)}, f32[128]{0:T(128)}, u32[]{:S(2)}) copy-start(f32[128]{0:T(128)} %copy-done.64) | copy-start | bytes 1540
  303.3 11.3 %all-to-all-start.2 = ((bf16[32,2,216]{2,1,0:T(2,128)(2,1)}), bf16[32,2,216]{2,1,0:T(2,128)(2,1)S(1)}, u32[]{:S(2)}, u32[]{:S(2)}) async-start(bf16[32,2,216]{2,1,0:T(2,128)(2,1)} %reshape.326), calls=%async_computation.3 | async-start | bytes 65536 | tf_op jit(solution)/shard_map/all_to_all | solution.py:373
  314.6 13.9 %all-to-all-start.4 = ((f32[32,1,504]{2,1,0:T(1,128)}), f32[32,1,504]{2,1,0:T(1,128)S(1)}, u32[]{:S(2)}, u32[]{:S(2)}) async-start(f32[32,1,504]{2,1,0:T(1,128)} %all_to_all.52), calls=%async_computation.5 | async-start | bytes 131072 | tf_op jit(solution)/shard_map/all_to_all | solution.py:397
  318.9 13.1 %copy-start.41 = (bf16[32,1,1152]{2,1,0:T(2,128)(2,1)S(1)}, bf16[32,1,1152]{2,1,0:T(2,128)(2,1)}, u32[]{:S(2)}) copy-start(bf16[32,1,1152]{2,1,0:T(2,128)(2,1)} %copy-done.40) | copy-start | bytes 221188
  328.5 12.1 %all-to-all-start.3 = ((f32[16,1,1152]{2,1,0:T(1,128)}), f32[16,1,1152]{2,1,0:T(1,128)S(1)}, u32[]{:S(2)}, u32[]{:S(2)}) async-start(f32[16,1,1152]{2,1,0:T(1,128)} %copy.287), calls=%async_computation.4 | async-start | bytes 147456 | tf_op jit(solution)/shard_map/all_to_all | solution.py:379
  332.5 63.8 %copy-start.1 = (f32[432,1152]{1,0:T(8,128)}, f32[432,1152]{1,0:T(8,128)S(1)}, u32[]{:S(2)}) copy-start(f32[432,1152]{1,0:T(8,128)S(1)} %fusion.72.refs_0_) | copy-start | bytes 5971972
  332.5 60.2 %copy-start.55 = (f32[1,1152]{1,0:T(1,128)S(1)}, f32[1,1152]{1,0:T(1,128)}, u32[]{:S(2)}) copy-start(f32[1,1152]{1,0:T(1,128)} %get-tuple-element.124) | copy-start | bytes 13828
  332.5 60.2 %copy-start.56 = (f32[1,1152]{1,0:T(1,128)S(1)}, f32[1,1152]{1,0:T(1,128)}, u32[]{:S(2)}) copy-start(f32[1,1152]{1,0:T(1,128)} %get-tuple-element.125) | copy-start | bytes 13828
  388.5 11.7 %all-to-all-start.5 = ((f32[32,1,505]{2,1,0:T(1,128)}), f32[32,1,505]{2,1,0:T(1,128)S(1)}, u32[]{:S(2)}, u32[]{:S(2)}) async-start(f32[32,1,505]{2,1,0:T(1,128)} %broadcast_in_dim.118), calls=%async_computation.6 | async-start | bytes 131072 | tf_op jit(solution)/shard_map/all_to_all | solution.py:209
  393.3 23.8 %collective-permute-start.19 = (bf16[72,4672]{1,0:T(8,128)(2,1)}, bf16[72,4672]{1,0:T(8,128)(2,1)S(1)}, u32[]{:S(2)}, u32[]{:S(2)}) collective-permute-start(bf16[72,4672]{1,0:T(8,128)(2,1)} %reduce-scatter.7.cloned.1.call-done.refs_0_), channel_id=1, source_target_pairs={{0,16},{16,0},{1,17},{17,1},{2,18},{18,2},{3,19},{19,3},{4,20},{20... | collective-permute-start | bytes 2018312 | tf_op jit(solution)/shard_map/ppermute | solution.py:196
  407.7 8.7 %copy-start.51 = (f32[16128]{0:T(1024)S(1)}, f32[16128]{0:T(1024)}, u32[]{:S(2)}) copy-start(f32[16128]{0:T(1024)} %param.43) | copy-start | bytes 193540
  (54 other events, 215.2 us)
Sparse Core Ops, SparseCore 0:
  15.1 102.5 all-gather.2
  120.4 54.5 all-gather.4
  179.0 76.6 reduce-scatter.4
  259.7 125.2 reduce-scatter.6
